TPU v7x, 768 devices: a whole 4x8x12 slice. The times are simulated.
768 devices in a mesh: lat: 16 (over y, core), lon: 48 (over x, z).
Axes of the slice: x: 4, y: 8, z: 12, core: 2. Of those that a mesh axis runs over, the one named last changes fastest.
Arguments:
- features: bfloat16 [64, 256, 6144], P(None, 'lat', 'lon'), may hold values from -6 to 6
- labels: int32 [256, 6144], P('lat', 'lon'), may hold values from 0 to 5
- tile_regions: int32 [16, 48, 6], P('lat', 'lon'), may hold values from 0 to 5375, as said below
- bank_slot: int32 [5376], replicated, may hold values from 0 to 5375, as said below
- kernel_bank: bfloat16 [5376, 32, 512], P('lon'), may hold values from -0.25 to 0.25
- in_factor: bfloat16 [32, 64], replicated, may hold values from -0.75 to 0.75
- tap_factor: bfloat16 [16, 25], replicated, may hold values from -1.25 to 1.25
- out_factor: bfloat16 [64, 32], replicated, may hold values from -1 to 1
- out_bias: float32 [64], replicated, may hold values from -4 to 4
Outputs:
- mixed: bfloat16 [64, 256, 6144], P(None, 'lat', 'lon')
Inputs may be any that keep to these rules, and one draw needn't show every extreme that they name: `tile_regions`: each tile lists 6 distinct regions: exactly 2 held by the bank device of its own lon index, 2 by that of the next lon index and 2 by that of the previous one (lon indices wrap); within one latitude band the tiles ask each bank device for exactly 4 distinct regions in all. A permutation: region r is bank row bank_slot[r], held by the lon device bank_slot[r] // 112.
All inputs are finite; a program needn't handle non-finite values.
Results may differ from a plain program's by a relative error of at most 0.0056.
Values may be sent and summed in bfloat16 or wider, within the bound.
A program may use at most 32 MiB of HBM per device.

v0:
```python
import jax
import jax.numpy as jnp
from jax import lax
from jax.sharding import PartitionSpec as P

KS = 5
CAPU = 4
MAXR = 6


def extended(cells, sides, width, closed):
    for axis, dim in sides:
        count = lax.axis_size(axis)
        ends = count if closed else count - 1
        head = lax.slice_in_dim(cells, 0, width, axis=dim)
        tail = lax.slice_in_dim(cells, cells.shape[dim] - width, cells.shape[dim], axis=dim)
        cells = jnp.concatenate(
            [
                lax.ppermute(tail, axis, [(i, (i + 1) % count) for i in range(ends)]),
                cells,
                lax.ppermute(head, axis, [((i + 1) % count, i) for i in range(ends)]),
            ],
            axis=dim,
        )
    return cells


def shifted(value, axis, steps):
    count = lax.axis_size(axis)
    pairs = [(source, (source + steps) % count) for source in range(count)]
    return lax.ppermute(value, axis, pairs)


def tile_layer(window, tile_labels, region_cores, tap_factor, out_factor, out_bias):
    lat_len = window.shape[1] - KS + 1
    lon_len = window.shape[2] - KS + 1
    columns = jnp.stack([window[:, :, col_off : col_off + lon_len] for col_off in range(KS)])
    total = jnp.zeros((tap_factor.shape[0], window.shape[0] * lat_len * lon_len), jnp.float32)
    for row_off in range(KS):
        piece = columns[:, :, row_off : row_off + lat_len, :].reshape(KS, -1)
        weights = tap_factor[:, row_off * KS : (row_off + 1) * KS]
        total = total + jnp.dot(weights, piece, preferred_element_type=jnp.float32)
    tapped = total.astype(jnp.bfloat16).reshape(-1, lat_len * lon_len)
    tucker_rank = region_cores.shape[1]
    list_len = region_cores.shape[0]
    flat_cores = region_cores.reshape(list_len * tucker_rank, -1)
    all_regions = jnp.dot(flat_cores, tapped, preferred_element_type=jnp.float32).reshape(
        list_len, tucker_rank, -1
    )
    onehot = (
        tile_labels.reshape(-1)[None, :] == jnp.arange(list_len, dtype=jnp.int32)[:, None]
    ).astype(jnp.float32)
    hidden = jnp.sum(all_regions * onehot[:, None, :], axis=0).astype(jnp.bfloat16)
    output = jnp.dot(out_factor, hidden, preferred_element_type=jnp.float32) + out_bias[:, None]
    return jax.nn.silu(output).astype(jnp.bfloat16).reshape(-1, lat_len, lon_len)


def extend_rims(field_part):
    widened = extended(field_part, (("lon", 2),), KS // 2, True)
    return extended(widened, (("lat", 1),), KS // 2, False)


def project_in(in_factor, field_part):
    channels = field_part.shape[0]
    flat = field_part.reshape(channels, -1)
    reduced = jnp.dot(in_factor, flat, preferred_element_type=jnp.float32).astype(jnp.bfloat16)
    return reduced.reshape(in_factor.shape[0], field_part.shape[1], field_part.shape[2])


def on_device(
    features,
    labels,
    tile_regions,
    bank_slot,
    kernel_bank,
    in_factor,
    tap_factor,
    out_factor,
    out_bias,
):
    window = project_in(in_factor, extend_rims(features))
    held_rows = kernel_bank.shape[0]
    core_width = kernel_bank.shape[1] * kernel_bank.shape[2]
    flat_bank = kernel_bank.reshape(held_rows, core_width)
    lon_count = lax.axis_size("lon")
    myself = lax.axis_index("lon")
    own_list = tile_regions.reshape(1, MAXR)
    requests = lax.all_gather(own_list, "lon", axis=0, tiled=True)
    slot_all = bank_slot[requests.reshape(-1)]
    owner_all = slot_all // held_rows
    local_all = slot_all % held_rows
    prev_owner = (myself + lon_count - 1) % lon_count
    owner_hit = (owner_all[:, None] == jnp.arange(lon_count, dtype=jnp.int32)[None, :]).astype(
        jnp.float32
    )
    local_hit = (local_all[:, None] == jnp.arange(held_rows, dtype=jnp.int32)[None, :]).astype(
        jnp.float32
    )
    present = jnp.dot(owner_hit.T, local_hit) > 0.5
    position_all = jnp.cumsum(present.astype(jnp.int32), axis=1) - 1
    mine_present = lax.dynamic_index_in_dim(present, myself, 0, keepdims=False)
    mine_position = lax.dynamic_index_in_dim(position_all, myself, 0, keepdims=False)
    pick_rows = (
        mine_present[None, :]
        & (mine_position[None, :] == jnp.arange(CAPU, dtype=jnp.int32)[:, None])
    ).astype(jnp.bfloat16)
    packed = jnp.dot(pick_rows, flat_bank, preferred_element_type=jnp.float32).astype(jnp.bfloat16)
    own_slot = bank_slot[own_list.reshape(-1)]
    own_owner = own_slot // held_rows
    own_local = own_slot % held_rows
    own_position = position_all[own_owner, own_local]
    from_prev = shifted(packed, "lon", 1)
    from_next = shifted(packed, "lon", -1)
    candidates = jnp.concatenate([packed, from_prev, from_next], axis=0)
    block = jnp.where(own_owner == myself, 0, jnp.where(own_owner == prev_owner, 1, 2))
    column = block * CAPU + own_position
    choose_cols = (column[:, None] == jnp.arange(3 * CAPU, dtype=jnp.int32)[None, :]).astype(
        jnp.bfloat16
    )
    region_cores = jnp.dot(choose_cols, candidates, preferred_element_type=jnp.float32)
    region_cores = region_cores.astype(jnp.bfloat16).reshape(
        MAXR, kernel_bank.shape[1], kernel_bank.shape[2]
    )
    return tile_layer(window, labels, region_cores, tap_factor, out_factor, out_bias)


def solution(mesh):
    placed = (
        P(None, "lat", "lon"),
        P("lat", "lon"),
        P("lat", "lon", None),
        P(),
        P("lon", None, None),
        P(),
        P(),
        P(),
        P(),
    )
    return jax.shard_map(
        on_device, mesh=mesh, in_specs=placed, out_specs=P(None, "lat", "lon"), check_vma=False
    )
```

profile of v0, /device:TPU:1, one launch (start us, length us, event | category | flops | bytes accessed | tf_op | source)
XLA Modules:
  0.0 121.2 jit_solution(1535537388554232192)
XLA Ops:
  0.0 0.0 copy-start
  0.0 53.1 %all-gather = s32[48,1,6]{2,1,0:T(1,128)S(1)} all-gather(s32[1,1,6]{2,1,0:T(1,128)} %param.11), channel_id=2, replica_groups=mesh['lat'=16,'lon'=48] {'lon'}, dimensions={0}, use_global_device_ids=true | all-gather | bytes 1176 | tf_op jit(solution)/shard_map/all_gather | solution.py:88
  53.1 0.5 broadcast.284
  53.6 0.7 reduce.5
  54.3 0.1 reshape.213
  54.5 0.0 copy-done
  54.5 2.2 %gather_fusion.1 = s32[288]{0:T(512)S(1)} fusion(s32[5376]{0:T(1024)S(1)} %copy-done, s32[1024]{0:T(1024)S(1)} %pad_clamp_fusion), kind=kCustom, calls=%fused_computation.1 | custom fusion | bytes 3456 | tf_op jit(solution)/shard_map/gather | solution.py:89
  56.7 0.3 fusion.58
  57.1 0.3 reduce_window_sum.11
  57.4 4.5 %copy.10 = bf16[14,8,32,512]{3,1,2,0:T(8,128)(2,1)S(1)} copy(bf16[14,8,32,512]{3,2,1,0:T(8,128)(2,1)} %bitcast.105) | data formatting | bytes 7340032
  61.9 0.0 copy-start.1
  61.9 0.0 copy-start.5
  61.9 0.0 copy-start.4
  61.9 0.6 convolution_convert_fusion.1
  62.5 0.0 copy-start.3
  62.5 2.9 %collective-permute-start = (bf16[4,16384]{1,0:T(4,128)(2,1)S(1)}, bf16[4,16384]{1,0:T(4,128)(2,1)S(1)}, u32[]{:S(2)}, u32[]{:S(2)}) collective-permute-start(bf16[4,16384]{1,0:T(4,128)(2,1)S(1)} %convolution_convert_fusion.1), channel_id=1, source_target_pairs={{0,1},{1,2},{2,3},{3,4},{4,5},{5,6},{6,7},{7,8},{8,9},{9,10},{10,1... | collective-permute-start | bytes 393224 | tf_op jit(solution)/shard_map/ppermute | solution.py:31
  65.4 5.8 %collective-permute-start.1 = (bf16[4,16384]{1,0:T(4,128)(2,1)S(1)}, bf16[4,16384]{1,0:T(4,128)(2,1)S(1)}, u32[]{:S(2)}, u32[]{:S(2)}) collective-permute-start(bf16[4,16384]{1,0:T(4,128)(2,1)S(1)} %convolution_convert_fusion.1), channel_id=1, source_target_pairs={{0,47},{1,0},{2,1},{3,2},{4,3},{5,4},{6,5},{7,6},{8,7},{9,8},{10,9... | collective-permute-start | bytes 393224 | tf_op jit(solution)/shard_map/ppermute | solution.py:31
  71.2 0.0 copy-done.1
  71.2 0.1 fusion.57
  71.4 1.9 %collective-permute-start.2 = (bf16[64,16,2]{2,1,0:T(8,128)(2,1)S(1)}, bf16[64,16,2]{2,1,0:T(8,128)(2,1)S(1)}, u32[]{:S(2)}, u32[]{:S(2)}) collective-permute-start(bf16[64,16,2]{2,1,0:T(8,128)(2,1)S(1)} %get-tuple-element.12), channel_id=1, source_target_pairs={{0,1},{1,2},{2,3},{3,4},{4,5},{5,6},{6,7},{7,8},{8,9},{9,10},{10,1... | collective-permute-start | bytes 12296 | tf_op jit(solution)/shard_map/ppermute | solution.py:19
  73.3 6.7 %collective-permute-start.3 = (bf16[64,16,2]{2,1,0:T(8,128)(2,1)S(1)}, bf16[64,16,2]{2,1,0:T(8,128)(2,1)S(1)}, u32[]{:S(2)}, u32[]{:S(2)}) collective-permute-start(bf16[64,16,2]{2,1,0:T(8,128)(2,1)S(1)} %get-tuple-element.13), channel_id=1, source_target_pairs={{1,0},{2,1},{3,2},{4,3},{5,4},{6,5},{7,6},{8,7},{9,8},{10,9},{11,1... | collective-permute-start | bytes 12296 | tf_op jit(solution)/shard_map/ppermute | solution.py:21
  80.0 0.0 copy-done.5
  80.0 0.6 gather_fusion
  80.7 0.0 copy-done.4
  80.7 0.7 gather_fusion.2
  81.4 0.4 collective-permute-done.2
  81.8 1.5 %collective-permute-done.3 = bf16[64,16,2]{2,1,0:T(8,128)(2,1)S(1)} collective-permute-done((bf16[64,16,2]{2,1,0:T(8,128)(2,1)S(1)}, bf16[64,16,2]{2,1,0:T(8,128)(2,1)S(1)}, u32[]{:S(2)}, u32[]{:S(2)}) %collective-permute-start.3) | collective-permute-done | bytes 4128 | tf_op jit(solution)/shard_map/ppermute | solution.py:21
  83.3 0.4 pad_maximum_fusion.3
  83.7 18.6 %collective-permute-start.4 = (bf16[64,2,132]{2,1,0:T(2,128)(2,1)S(1)}, bf16[64,2,132]{2,1,0:T(2,128)(2,1)S(1)}, u32[]{:S(2)}, u32[]{:S(2)}) collective-permute-start(bf16[64,2,132]{2,1,0:T(2,128)(2,1)S(1)} %get-tuple-element.10), channel_id=1, source_target_pairs={{0,48},{48,96},{96,144},{144,192},{192,240},{240,288},{288,336},{3... | collective-permute-start | bytes 101384 | tf_op jit(solution)/shard_map/ppermute | solution.py:19
  102.3 2.1 %collective-permute-start.5 = (bf16[64,2,132]{2,1,0:T(2,128)(2,1)S(1)}, bf16[64,2,132]{2,1,0:T(2,128)(2,1)S(1)}, u32[]{:S(2)}, u32[]{:S(2)}) collective-permute-start(bf16[64,2,132]{2,1,0:T(2,128)(2,1)S(1)} %get-tuple-element.11), channel_id=1, source_target_pairs={{48,0},{96,48},{144,96},{192,144},{240,192},{288,240},{336,288},{3... | collective-permute-start | bytes 101384 | tf_op jit(solution)/shard_map/ppermute | solution.py:21
  104.5 0.0 collective-permute-done.4
  104.5 3.4 %collective-permute-done.5 = bf16[64,2,132]{2,1,0:T(2,128)(2,1)S(1)} collective-permute-done((bf16[64,2,132]{2,1,0:T(2,128)(2,1)S(1)}, bf16[64,2,132]{2,1,0:T(2,128)(2,1)S(1)}, u32[]{:S(2)}, u32[]{:S(2)}) %collective-permute-start.5) | collective-permute-done | bytes 33824 | tf_op jit(solution)/shard_map/ppermute | solution.py:21
  107.9 0.8 pad_maximum_fusion
  108.8 0.6 reshape.215
  109.3 0.0 copy-done.3
  109.3 0.2 fusion.2
  109.5 0.5 reshape.216
  110.0 0.2 fusion.27
  110.2 0.2 fusion.26
  110.4 0.0 copy-start.2
  110.4 0.2 fusion.25
  110.5 0.2 fusion.24
  110.7 0.8 fusion.56
  111.5 0.0 copy-done.2
  111.5 0.7 fusion.13
  112.2 0.8 convolution_add_fusion.3
  113.0 0.9 convolution_add_fusion.2
  113.9 0.8 convolution_add_fusion.1
  114.7 0.8 fusion.1
  115.4 0.0 copy-start.6
  115.5 0.0 copy-start.7
  115.5 2.0 %reshape.248 = bf16[512,2048,1]{1,0,2:T(8,128)(2,1)} reshape(bf16[16,65536]{1,0:T(8,128)(2,1)S(1)} %fusion.1) | data formatting | bytes 4194304 | tf_op jit(solution)/shard_map/reshape | solution.py:43
  117.5 0.0 collective-permute-done
  117.5 0.0 collective-permute-done.1
  117.5 0.4 convolution_convert_fusion
  117.9 2.2 %fusion.4 = bf16[32,2048]{1,0:T(8,128)(2,1)S(1)} fusion(bf16[512,2048,1]{1,0,2:T(8,128)(2,1)} %reshape.248, f32[6,2048]{1,0:T(8,128)S(1)} %fusion.32, bf16[1,6,32,512]{3,1,2,0:T(8,128)(2,1)S(1)} %bitcast.107), kind=kOutput, calls=%fused_computation.16 | convolution fusion | flops 403374080 | bytes 2473984 | tf_op jit(solution)/shard_map/dot_general | solution.py:47
  120.0 0.0 copy-done.6
  120.1 0.0 copy-done.7
  120.1 0.3 fusion.21
  120.4 0.7 copy.17
  (12 shorter events, 0.2 us)
Async XLA Ops:
  0.0 54.5 %copy-start = (s32[5376]{0:T(1024)S(1)}, s32[5376]{0:T(1024)}, u32[]{:S(2)}) copy-start(s32[5376]{0:T(1024)} %param.12) | copy-start | bytes 64516
  61.9 9.4 %copy-start.1 = (bf16[64,16,128]{2,1,0:T(8,128)(2,1)S(1)}, bf16[64,16,128]{2,1,0:T(8,128)(2,1)}, u32[]{:S(2)}) copy-start(bf16[64,16,128]{2,1,0:T(8,128)(2,1)} %param.9) | copy-start | bytes 786436
  61.9 18.1 %copy-start.5 = (s32[1,1,6]{2,1,0:T(1,128)S(1)}, s32[1,1,6]{2,1,0:T(1,128)}, u32[]{:S(2)}) copy-start(s32[1,1,6]{2,1,0:T(1,128)} %param.11) | copy-start | bytes 76
  61.9 18.8 %copy-start.4 = (s32[16,128]{1,0:T(8,128)S(1)}, s32[16,128]{1,0:T(8,128)}, u32[]{:S(2)}) copy-start(s32[16,128]{1,0:T(8,128)} %param.10) | copy-start | bytes 24580
  62.5 46.9 %copy-start.3 = (bf16[32,64]{1,0:T(8,128)(2,1)S(1)}, bf16[32,64]{1,0:T(8,128)(2,1)}, u32[]{:S(2)}) copy-start(bf16[32,64]{1,0:T(8,128)(2,1)} %param.14) | copy-start | bytes 12292
  62.5 55.0 %collective-permute-start = (bf16[4,16384]{1,0:T(4,128)(2,1)S(1)}, bf16[4,16384]{1,0:T(4,128)(2,1)S(1)}, u32[]{:S(2)}, u32[]{:S(2)}) collective-permute-start(bf16[4,16384]{1,0:T(4,128)(2,1)S(1)} %convolution_convert_fusion.1), channel_id=1, source_target_pairs={{0,1},{1,2},{2,3},{3,4},{4,5},{5,6},{6,7},{7,8},{8,9},{9,10},{10,1... | collective-permute-start | bytes 393224 | tf_op jit(solution)/shard_map/ppermute | solution.py:31
  65.4 52.1 %collective-permute-start.1 = (bf16[4,16384]{1,0:T(4,128)(2,1)S(1)}, bf16[4,16384]{1,0:T(4,128)(2,1)S(1)}, u32[]{:S(2)}, u32[]{:S(2)}) collective-permute-start(bf16[4,16384]{1,0:T(4,128)(2,1)S(1)} %convolution_convert_fusion.1), channel_id=1, source_target_pairs={{0,47},{1,0},{2,1},{3,2},{4,3},{5,4},{6,5},{7,6},{8,7},{9,8},{10,9... | collective-permute-start | bytes 393224 | tf_op jit(solution)/shard_map/ppermute | solution.py:31
  71.4 10.4 %collective-permute-start.2 = (bf16[64,16,2]{2,1,0:T(8,128)(2,1)S(1)}, bf16[64,16,2]{2,1,0:T(8,128)(2,1)S(1)}, u32[]{:S(2)}, u32[]{:S(2)}) collective-permute-start(bf16[64,16,2]{2,1,0:T(8,128)(2,1)S(1)} %get-tuple-element.12), channel_id=1, source_target_pairs={{0,1},{1,2},{2,3},{3,4},{4,5},{5,6},{6,7},{7,8},{8,9},{9,10},{10,1... | collective-permute-start | bytes 12296 | tf_op jit(solution)/shard_map/ppermute | solution.py:19
  73.3 10.0 %collective-permute-start.3 = (bf16[64,16,2]{2,1,0:T(8,128)(2,1)S(1)}, bf16[64,16,2]{2,1,0:T(8,128)(2,1)S(1)}, u32[]{:S(2)}, u32[]{:S(2)}) collective-permute-start(bf16[64,16,2]{2,1,0:T(8,128)(2,1)S(1)} %get-tuple-element.13), channel_id=1, source_target_pairs={{1,0},{2,1},{3,2},{4,3},{5,4},{6,5},{7,6},{8,7},{9,8},{10,9},{11,1... | collective-permute-start | bytes 12296 | tf_op jit(solution)/shard_map/ppermute | solution.py:21
  83.7 20.8 %collective-permute-start.4 = (bf16[64,2,132]{2,1,0:T(2,128)(2,1)S(1)}, bf16[64,2,132]{2,1,0:T(2,128)(2,1)S(1)}, u32[]{:S(2)}, u32[]{:S(2)}) collective-permute-start(bf16[64,2,132]{2,1,0:T(2,128)(2,1)S(1)} %get-tuple-element.10), channel_id=1, source_target_pairs={{0,48},{48,96},{96,144},{144,192},{192,240},{240,288},{288,336},{3... | collective-permute-start | bytes 101384 | tf_op jit(solution)/shard_map/ppermute | solution.py:19
  102.3 5.6 %collective-permute-start.5 = (bf16[64,2,132]{2,1,0:T(2,128)(2,1)S(1)}, bf16[64,2,132]{2,1,0:T(2,128)(2,1)S(1)}, u32[]{:S(2)}, u32[]{:S(2)}) collective-permute-start(bf16[64,2,132]{2,1,0:T(2,128)(2,1)S(1)} %get-tuple-element.11), channel_id=1, source_target_pairs={{48,0},{96,48},{144,96},{192,144},{240,192},{288,240},{336,288},{3... | collective-permute-start | bytes 101384 | tf_op jit(solution)/shard_map/ppermute | solution.py:21
  110.4 1.2 copy-start.2
  115.4 4.6 %copy-start.6 = (bf16[64,32]{0,1:T(8,128)(2,1)S(1)}, bf16[64,32]{0,1:T(8,128)(2,1)}, u32[]{:S(2)}) copy-start(bf16[64,32]{0,1:T(8,128)(2,1)} %param.16) | copy-start | bytes 12292
  115.5 4.6 %copy-start.7 = (f32[64]{0:T(128)S(1)}, f32[64]{0:T(128)}, u32[]{:S(2)}) copy-start(f32[64]{0:T(128)} %param.17) | copy-start | bytes 772
where the time goes:
time: 123 us; the launch traced here: 121 us
  blocking collectives  53.1 us (43%)
  starting transfers between devices  38.1 us (31%)
  local copies, waits for them, and re-layouts  14.1 us (11%)
  matrix products  7.82 us (6%)
  waiting for transfers between devices  5.36 us (4%)
  other arithmetic  2.32 us (2%)
    all_gather x1, blocking collectives, on_device(): requests = lax.all_gather(own_list, 'lon', axis=0, tiled=True)  53.1 us
    ppermute x2, starting transfers between devices, extended(): lax.ppermute(tail, axis, [(i, (i + 1) % count) for i in range(ends)])  20.6 us
    ppermute x2, starting transfers between devices, extended(): lax.ppermute(head, axis, [((i + 1) % count, i) for i in range(ends)])  8.78 us
    ppermute x2, starting transfers between devices, shifted(): return lax.ppermute(value, axis, pairs)  8.72 us
    unnamed x22, local copies, waits for them, and re-layouts  5.76 us
    ppermute x2, waiting for transfers between devices, extended(): lax.ppermute(head, axis, [((i + 1) % count, i) for i in range(ends)])  4.92 us
    dot_general x5, matrix products, tile_layer(): total = total + jnp.dot(weights, piece, preferred_element_type=jnp.float32)  3.86 us
  transfers between devices with their start and end apart: 6, of which 3 were waited for; matrix products, arithmetic and copies ran while one was open for 9% of the time, Pallas kernels for 0%

commit v1 on v0

v1 whole, which is shorter than its diff:
```python
import functools

import jax
import jax.numpy as jnp
from jax import lax
from jax.experimental import pallas as pl
from jax.experimental.pallas import tpu as pltpu
from jax.sharding import PartitionSpec as P

KS = 5
REACH = KS // 2
LANES = 128
MAXR = 6
BF16 = jnp.bfloat16
F32 = jnp.float32
MESH = pl.DeviceIdType.MESH


def dot(a, b):
    return jnp.dot(a, b, preferred_element_type=F32)


def kernel(
    n_lat, n_lon,
    feat_h, lab_h, tr_h, slot_h, bank_h, inf_h, tap_h, outf_h, bias_h,
    out_ref,
    feat_v, lab_v, tr_s, slot_s, bank_v, inf_v, tap_v, outf_v, bias_v,
    ask_s, asked_s, spread, red, pack, packs, tops, bots, send_cores, cores,
    kron, moved, tapped, held, local_sem, send_sem, recv_sem,
):
    lat, lon = lax.axis_index("lat"), lax.axis_index("lon")
    up, down = lax.rem(lat + (n_lat - 1), n_lat), lax.rem(lat + 1, n_lat)
    prev, nxt = lax.rem(lon + (n_lon - 1), n_lon), lax.rem(lon + 1, n_lon)
    channels, rows, _ = feat_v.shape
    rank = inf_v.shape[0]
    taps_rank = tap_v.shape[0]
    bank_rows = bank_v.shape[0]
    around = [(lat, prev), (lat, nxt), (up, lon), (down, lon), (up, prev), (up, nxt), (down, prev), (down, nxt)]

    barrier = pltpu.get_barrier_semaphore()
    for place in around:
        pl.semaphore_signal(barrier, inc=1, device_id=place, device_id_type=MESH)

    def local(source, target, index):
        copy = pltpu.make_async_copy(source, target, local_sem.at[index])
        copy.start()
        return copy

    get_tr = local(tr_h, tr_s, 0)
    get_slot = local(slot_h, slot_s, 1)
    get_feat = local(feat_h, feat_v, 2)
    get_inf = local(inf_h, inf_v, 3)
    get_tap = local(tap_h, tap_v, 4)
    get_lab = local(lab_h, lab_v, 5)
    get_outf = local(outf_h, outf_v, 6)
    get_bias = local(bias_h, bias_v, 7)
    part = bank_rows // 4
    get_bank = [
        local(bank_h.at[pl.ds(i * part, part)], bank_v.at[pl.ds(i * part, part)], 8 + i) for i in range(4)
    ]

    def remote(source, target, index, place):
        return pltpu.make_async_remote_copy(
            src_ref=source, dst_ref=target, send_sem=send_sem.at[index], recv_sem=recv_sem.at[index],
            device_id=place, device_id_type=MESH,
        )

    get_tr.wait()
    get_slot.wait()
    slots = [slot_s[tr_s[0, 0, j]] for j in range(MAXR)]

    def wanted(owner):
        first = owner * bank_rows
        row_a = row_b = at_a = at_b = count = jnp.int32(0)
        for j in range(MAXR):
            row = slots[j] - first
            hit = (row >= 0) & (row < bank_rows)
            is_a = hit & (count == 0)
            is_b = hit & (count == 1)
            row_a, at_a = jnp.where(is_a, row, row_a), jnp.where(is_a, j, at_a)
            row_b, at_b = jnp.where(is_b, row, row_b), jnp.where(is_b, j, at_b)
            count = count + hit.astype(jnp.int32)
        return row_a, row_b, at_a, at_b

    own_a, own_b, own_at, _ = wanted(lon)
    prev_a, prev_b, prev_at_a, prev_at_b = wanted(prev)
    next_a, next_b, next_at_a, next_at_b = wanted(nxt)
    ask_s[0, 0], ask_s[0, 1] = prev_a, prev_b
    ask_s[1, 0], ask_s[1, 1] = next_a, next_b

    pl.semaphore_wait(barrier, len(around))
    ask_prev = remote(ask_s.at[0], asked_s.at[1], 0, (lat, prev))
    ask_next = remote(ask_s.at[1], asked_s.at[0], 1, (lat, nxt))
    ask_prev.start()
    ask_next.start()

    get_feat.wait()
    get_inf.wait()
    spread[...] = feat_v[...].astype(F32).reshape(channels * rows, LANES)
    lane = lax.broadcasted_iota(jnp.int32, (rank, LANES), 1)
    packed = jnp.zeros((rank, LANES), F32)
    weights = inf_v[...]
    for r in range(rows):
        columns = spread[pl.ds(r, channels, stride=rows), :].astype(BF16)
        block = dot(weights, columns).astype(BF16)
        red[:, r * LANES : (r + 1) * LANES] = block
        rolled = pltpu.roll(block.astype(F32), (4 * r + 2) % LANES, 1)
        packed = jnp.where((lane >= 4 * r) & (lane < 4 * r + 4), rolled, packed)
    pack[...] = packed.astype(BF16)

    edge = REACH * LANES
    whole = rows * LANES
    rims = [
        remote(pack, packs.at[1], 2, (lat, prev)),
        remote(pack, packs.at[0], 3, (lat, nxt)),
        remote(red.at[:, pl.ds(0, edge)], bots, 4, (up, lon)),
        remote(red.at[:, pl.ds(whole - edge, edge)], tops, 5, (down, lon)),
        remote(pack, packs.at[5], 6, (up, prev)),
        remote(pack, packs.at[4], 7, (up, nxt)),
        remote(pack, packs.at[3], 8, (down, prev)),
        remote(pack, packs.at[2], 9, (down, nxt)),
    ]
    for copy in rims:
        copy.start()

    for copy in get_bank:
        copy.wait()
    ask_prev.wait_recv()
    send_cores[0] = bank_v[asked_s[1, 0]]
    send_cores[1] = bank_v[asked_s[1, 1]]
    ask_next.wait_recv()
    send_cores[2] = bank_v[asked_s[0, 0]]
    send_cores[3] = bank_v[asked_s[0, 1]]
    give_next = remote(send_cores.at[pl.ds(0, 2)], cores.at[pl.ds(0, 2)], 10, (lat, nxt))
    give_prev = remote(send_cores.at[pl.ds(2, 2)], cores.at[pl.ds(2, 2)], 11, (lat, prev))
    give_next.start()
    give_prev.start()

    get_tap.wait()
    depth = kron.shape[1]
    taps = tap_v.shape[1]
    pick = (
        lax.broadcasted_iota(jnp.int32, (taps, depth), 1) // rank == lax.broadcasted_iota(jnp.int32, (taps, depth), 0)
    ).astype(F32).astype(BF16)
    wide = dot(tap_v[...], pick)
    same = lax.broadcasted_iota(jnp.int32, (rank, depth), 1) % rank == lax.broadcasted_iota(jnp.int32, (rank, depth), 0)
    for c in range(taps_rank):
        kron[c * rank : (c + 1) * rank, :] = jnp.where(
            same, jnp.broadcast_to(wide[c : c + 1, :], (rank, depth)), 0.0
        ).astype(BF16)

    for copy in rims:
        copy.wait_recv()
    not_first = (lat > 0).astype(F32)
    not_last = (lat < n_lat - 1).astype(F32)
    even = lane % 4 < 2

    def place_row(at, block, sides, row):
        beside = pltpu.roll(sides, (LANES - 2 - 4 * row) % LANES, 1)
        shapes = (
            pltpu.roll(jnp.where(lane >= LANES - 2, beside, block), 2, 1),
            pltpu.roll(jnp.where(lane == LANES - 1, beside, block), 1, 1),
            block,
            pltpu.roll(jnp.where(lane == 0, beside, block), LANES - 1, 1),
            pltpu.roll(jnp.where(lane < 2, beside, block), LANES - 2, 1),
        )
        for dx in range(KS):
            moved[dx * rank : (dx + 1) * rank, at * LANES : (at + 1) * LANES] = shapes[dx].astype(BF16)

    middle = jnp.where(even, packs[0].astype(F32), packs[1].astype(F32))
    above = jnp.where(even, packs[2].astype(F32), packs[3].astype(F32)) * not_first
    below = jnp.where(even, packs[4].astype(F32), packs[5].astype(F32)) * not_last
    for r in range(REACH):
        lanes = pl.ds(r * LANES, LANES)
        place_row(r, tops[:, lanes].astype(F32) * not_first, above, rows - REACH + r)
        place_row(rows + REACH + r, bots[:, lanes].astype(F32) * not_last, below, r)
    for r in range(rows):
        place_row(REACH + r, red[:, r * LANES : (r + 1) * LANES].astype(F32), middle, r)

    get_lab.wait()
    own_cores = jnp.concatenate([bank_v[own_a], bank_v[own_b]], axis=0)
    span = 2 * LANES

    def label_of(i):
        return jnp.concatenate(
            [jnp.broadcast_to(lab_v[pl.ds(2 * i + k, 1), :], (rank, LANES)) for k in range(2)], axis=1
        )

    @pl.loop(0, rows // 2)
    def _(i):
        start = pl.multiple_of(i * span, span)
        pieces = [moved[:, pl.ds(pl.multiple_of(start + dy * LANES, LANES), span)] for dy in range(KS)]
        pieces.append(jnp.zeros((depth - KS * KS * rank, span), BF16))
        result = dot(kron[...], jnp.concatenate(pieces, axis=0)).astype(BF16)
        tapped[:, pl.ds(start, span)] = result
        ours = dot(own_cores, result)
        held[:, pl.ds(start, span)] = jnp.where(label_of(i) == own_at, ours[:rank], ours[rank:])

    get_outf.wait()
    get_bias.wait()
    square = (channels, channels)
    eye = lax.broadcasted_iota(jnp.int32, square, 0) == lax.broadcasted_iota(jnp.int32, square, 1)
    bias = jnp.sum(jnp.where(eye, jnp.broadcast_to(bias_v[...], square), 0.0), axis=1, keepdims=True)
    give_next.wait_recv()
    give_prev.wait_recv()
    others = cores[...].reshape(4 * rank, cores.shape[2])
    last = outf_v[...]

    @pl.loop(0, rows // 2)
    def _(i):
        start = pl.multiple_of(i * span, span)
        theirs = dot(others, tapped[:, pl.ds(start, span)])
        label = label_of(i)
        hidden = held[:, pl.ds(start, span)]
        for k, at in enumerate((prev_at_a, prev_at_b, next_at_a, next_at_b)):
            hidden = jnp.where(label == at, theirs[k * rank : (k + 1) * rank], hidden)
        value = dot(last, hidden.astype(BF16)) + bias
        value = value / (1.0 + jnp.exp(-value))
        for k in range(2):
            spread[pl.ds(2 * i + k, channels, stride=rows), :] = value[:, k * LANES : (k + 1) * LANES]

    out_ref[...] = spread[...].reshape(channels, rows, LANES).astype(BF16)

    ask_prev.wait_send()
    ask_next.wait_send()
    for copy in rims:
        copy.wait_send()
    give_next.wait_send()
    give_prev.wait_send()


def on_device(features, labels, tile_regions, bank_slot, kernel_bank, in_factor, tap_factor, out_factor, out_bias):
    n_lat, n_lon = lax.axis_size("lat"), lax.axis_size("lon")
    channels, rows, columns = features.shape
    rank = in_factor.shape[0]
    taps_rank, taps = tap_factor.shape
    bank_rows, _, width = kernel_bank.shape
    depth = -(-taps * rank // LANES) * LANES
    cells = rows * columns
    wide = (rows + 2 * REACH) * columns
    dma = pltpu.SemaphoreType.DMA
    anywhere = pl.BlockSpec(memory_space=pltpu.HBM)
    return pl.pallas_call(
        functools.partial(kernel, n_lat, n_lon),
        out_shape=jax.ShapeDtypeStruct(features.shape, BF16),
        in_specs=[anywhere] * 9,
        out_specs=pl.BlockSpec(memory_space=pltpu.VMEM),
        scratch_shapes=[
            pltpu.VMEM(features.shape, BF16),
            pltpu.VMEM(labels.shape, jnp.int32),
            pltpu.SMEM(tile_regions.shape, jnp.int32),
            pltpu.SMEM(bank_slot.shape, jnp.int32),
            pltpu.VMEM(kernel_bank.shape, BF16),
            pltpu.VMEM(in_factor.shape, BF16),
            pltpu.VMEM(tap_factor.shape, BF16),
            pltpu.VMEM(out_factor.shape, BF16),
            pltpu.VMEM((1, out_bias.shape[0]), F32),
            pltpu.SMEM((2, 2), jnp.int32),
            pltpu.SMEM((2, 2), jnp.int32),
            pltpu.VMEM((channels * rows, columns), F32),
            pltpu.VMEM((rank, cells), BF16),
            pltpu.VMEM((rank, columns), BF16),
            pltpu.VMEM((6, rank, columns), BF16),
            pltpu.VMEM((rank, REACH * columns), BF16),
            pltpu.VMEM((rank, REACH * columns), BF16),
            pltpu.VMEM((4, rank, width), BF16),
            pltpu.VMEM((4, rank, width), BF16),
            pltpu.VMEM((taps_rank * rank, depth), BF16),
            pltpu.VMEM((KS * rank, wide), BF16),
            pltpu.VMEM((taps_rank * rank, cells), BF16),
            pltpu.VMEM((rank, cells), F32),
            dma((12,)),
            dma((12,)),
            dma((12,)),
        ],
        compiler_params=pltpu.CompilerParams(
            collective_id=0, has_side_effects=True, vmem_limit_bytes=48 * 1024 * 1024
        ),
        name="layer",
    )(
        features, labels, tile_regions, bank_slot, kernel_bank, in_factor, tap_factor, out_factor,
        out_bias.reshape(1, -1),
    )


def solution(mesh):
    placed = (
        P(None, "lat", "lon"),
        P("lat", "lon"),
        P("lat", "lon", None),
        P(),
        P("lon", None, None),
        P(),
        P(),
        P(),
        P(),
    )
    return jax.shard_map(
        on_device, mesh=mesh, in_specs=placed, out_specs=P(None, "lat", "lon"), check_vma=False
    )
```

time: 123 us -> 40.1 us (0.33); the launches traced: 121 us -> 39.7 us
  blocking collectives: 53.1 us -> 0 us
  starting transfers between devices: 38.1 us -> 0 us
  Pallas kernels: 0 us -> 31.1 us
  matrix products: 7.82 us -> 0 us
  local copies, waits for them, and re-layouts: 14.1 us -> 8.6 us
  waiting for transfers between devices: 5.36 us -> 0 us
  other arithmetic: 2.32 us -> 0 us
    all_gather x1 -> x0, blocking collectives: 53.1 us -> none  [on_device(): requests = lax.all_gather(own_list, 'lon', axis=0, tiled=True)]
    ppermute x6 -> x0, starting transfers between devices: 38.1 us -> none  [the longest x2 20.6 us: extended(): lax.ppermute(tail, axis, [(i, (i + 1) % count) for i in range(ends)])]
    pallas_call x0 -> x1, Pallas kernels: none -> 31.1 us  [on_device(): pl.pallas_call(functools.partial(kernel, n_lat, n_lon), out_shape=jax.Sha...]
    dot_general x11 -> x0, matrix products: 7.82 us -> none  [the longest x5 3.86 us: tile_layer(): total = total + jnp.dot(weights, piece, preferred_element_type=jnp.float32)]
    ppermute x6 -> x0, waiting for transfers between devices: 5.36 us -> none  [the longest x2 4.92 us: extended(): lax.ppermute(head, axis, [((i + 1) % count, i) for i in range(ends)])]
    gather x3 -> x0, local copies, waits for them, and re-layouts: 3.52 us -> none  [the longest x1 2.23 us: on_device(): slot_all = bank_slot[requests.reshape(-1)]]
    reshape x4 -> x0, local copies, waits for them, and re-layouts: 3.17 us -> none  [the longest x1 2.02 us: tile_layer(): tapped = total.astype(jnp.bfloat16).reshape(-1, lat_len * lon_len)]
    unnamed x22 -> x18, local copies, waits for them, and re-layouts: 5.76 us -> 8.6 us
  transfers between devices with their start and end apart: 6 -> 0, of which waited for: 3 -> 0; matrix products, arithmetic and copies ran while one was open for 9% -> 0% of each run, Pallas kernels for 0% -> 0%
where the time goes in v1:
time: 40.1 us; the launch traced here: 39.7 us
  Pallas kernels  31.1 us (78%)
  local copies, waits for them, and re-layouts  8.6 us (21%)
    pallas_call x1, Pallas kernels, on_device(): pl.pallas_call(functools.partial(kernel, n_lat, n_lon), out_shape=jax.Sha...  31.1 us
    unnamed x18, local copies, waits for them, and re-layouts  8.6 us

profile of v1, /device:TPU:1, one launch (start us, length us, event | category | flops | bytes accessed | tf_op | source)
XLA Modules:
  0.0 39.7 jit_solution(17925685774412431134)
XLA Ops:
  0.0 0.8 %copy.10.outf_h = bf16[64,32]{1,0:T(8,128)(2,1)S(1)} copy(bf16[64,32]{0,1:T(8,128)(2,1)} %param.16) | data formatting | bytes 8192 | tf_op args[7]
  0.8 0.0 copy-start
  0.8 2.0 %copy-done = bf16[112,32,512]{2,1,0:T(8,128)(2,1)S(1)} copy-done((bf16[112,32,512]{2,1,0:T(8,128)(2,1)S(1)}, bf16[112,32,512]{2,1,0:T(8,128)(2,1)}, u32[]{:S(2)}) %copy-start) | copy-done | bytes 3670040
  2.8 0.0 copy-start.1
  2.8 0.9 %copy-done.1 = bf16[64,16,128]{2,1,0:T(8,128)(2,1)S(1)} copy-done((bf16[64,16,128]{2,1,0:T(8,128)(2,1)S(1)}, bf16[64,16,128]{2,1,0:T(8,128)(2,1)}, u32[]{:S(2)}) %copy-start.1) | copy-done | bytes 262168
  3.8 0.0 copy-start.2
  3.8 0.7 %copy-done.2 = s32[5376]{0:T(1024)S(1)} copy-done((s32[5376]{0:T(1024)S(1)}, s32[5376]{0:T(1024)}, u32[]{:S(2)}) %copy-start.2) | copy-done | bytes 21528
  4.5 0.0 copy-start.3
  4.5 0.7 %copy-done.3 = s32[16,128]{1,0:T(8,128)S(1)} copy-done((s32[16,128]{1,0:T(8,128)S(1)}, s32[16,128]{1,0:T(8,128)}, u32[]{:S(2)}) %copy-start.3) | copy-done | bytes 8216
  5.2 0.0 copy-start.4
  5.2 0.7 %copy-done.4 = bf16[32,64]{1,0:T(8,128)(2,1)S(1)} copy-done((bf16[32,64]{1,0:T(8,128)(2,1)S(1)}, bf16[32,64]{1,0:T(8,128)(2,1)}, u32[]{:S(2)}) %copy-start.4) | copy-done | bytes 4120
  5.9 0.0 copy-start.5
  5.9 0.7 %copy-done.5 = bf16[16,25]{1,0:T(8,128)(2,1)S(1)} copy-done((bf16[16,25]{1,0:T(8,128)(2,1)S(1)}, bf16[16,25]{1,0:T(8,128)(2,1)}, u32[]{:S(2)}) %copy-start.5) | copy-done | bytes 824
  6.6 0.0 copy-start.6
  6.6 0.7 %copy-done.6 = s32[1,1,6]{2,1,0:T(1,128)S(1)} copy-done((s32[1,1,6]{2,1,0:T(1,128)S(1)}, s32[1,1,6]{2,1,0:T(1,128)}, u32[]{:S(2)}) %copy-start.6) | copy-done | bytes 48
  7.3 0.0 copy-start.7
  7.3 0.7 %copy-done.7 = f32[64]{0:T(128)S(1)} copy-done((f32[64]{0:T(128)S(1)}, f32[64]{0:T(128)}, u32[]{:S(2)}) %copy-start.7) | copy-done | bytes 280
  7.9 31.1 %layer.1 = bf16[64,16,128]{2,1,0:T(8,128)(2,1)S(1)} custom-call(bf16[64,16,128]{2,1,0:T(8,128)(2,1)S(1)} %copy-done.1, s32[16,128]{1,0:T(8,128)S(1)} %copy-done.3, s32[1,1,6]{2,1,0:T(1,128)S(1)} %copy-done.6, s32[5376]{0:T(1024)S(1)} %copy-done.2, bf16[112,32,512]{2,1,0:T(8,128)(2,1)S(1)} %copy-done, bf16[32,64]{1,0:T(8,128)(2,1)S(1)} %copy-done.4, ...), custom_call_target="tpu_custom_call" | custom-call | tf_op jit(solution)/shard_map/layer/pallas_call | solution.py:243
  39.0 0.7 %copy.12 = bf16[64,16,128]{2,1,0:T(8,128)(2,1)} copy(bf16[64,16,128]{2,1,0:T(8,128)(2,1)S(1)} %layer.1) | data formatting | bytes 524288
Async XLA Ops:
  0.8 2.0 %copy-start = (bf16[112,32,512]{2,1,0:T(8,128)(2,1)S(1)}, bf16[112,32,512]{2,1,0:T(8,128)(2,1)}, u32[]{:S(2)}) copy-start(bf16[112,32,512]{2,1,0:T(8,128)(2,1)} %bank_h.1) | copy-start | bytes 11010052
  2.8 0.9 %copy-start.1 = (bf16[64,16,128]{2,1,0:T(8,128)(2,1)S(1)}, bf16[64,16,128]{2,1,0:T(8,128)(2,1)}, u32[]{:S(2)}) copy-start(bf16[64,16,128]{2,1,0:T(8,128)(2,1)} %feat_h.1) | copy-start | bytes 786436
  3.8 0.7 %copy-start.2 = (s32[5376]{0:T(1024)S(1)}, s32[5376]{0:T(1024)}, u32[]{:S(2)}) copy-start(s32[5376]{0:T(1024)} %slot_h.1) | copy-start | bytes 64516
  4.5 0.7 %copy-start.3 = (s32[16,128]{1,0:T(8,128)S(1)}, s32[16,128]{1,0:T(8,128)}, u32[]{:S(2)}) copy-start(s32[16,128]{1,0:T(8,128)} %lab_h.1) | copy-start | bytes 24580
  5.2 0.7 %copy-start.4 = (bf16[32,64]{1,0:T(8,128)(2,1)S(1)}, bf16[32,64]{1,0:T(8,128)(2,1)}, u32[]{:S(2)}) copy-start(bf16[32,64]{1,0:T(8,128)(2,1)} %inf_h.1) | copy-start | bytes 12292
  5.9 0.7 %copy-start.5 = (bf16[16,25]{1,0:T(8,128)(2,1)S(1)}, bf16[16,25]{1,0:T(8,128)(2,1)}, u32[]{:S(2)}) copy-start(bf16[16,25]{1,0:T(8,128)(2,1)} %tap_h.1) | copy-start | bytes 2404
  6.6 0.7 %copy-start.6 = (s32[1,1,6]{2,1,0:T(1,128)S(1)}, s32[1,1,6]{2,1,0:T(1,128)}, u32[]{:S(2)}) copy-start(s32[1,1,6]{2,1,0:T(1,128)} %tr_h.1) | copy-start | bytes 76
  7.3 0.7 %copy-start.7 = (f32[64]{0:T(128)S(1)}, f32[64]{0:T(128)}, u32[]{:S(2)}) copy-start(f32[64]{0:T(128)} %param.17) | copy-start | bytes 772

commit v2 on v1

--- a/solution.py
+++ b/solution.py
@@ -11,6 +11,7 @@
 REACH = KS // 2
 LANES = 128
 MAXR = 6
+WAVE = 12
 BF16 = jnp.bfloat16
 F32 = jnp.float32
 MESH = pl.DeviceIdType.MESH
@@ -26,7 +27,7 @@
     out_ref,
     feat_v, lab_v, tr_s, slot_s, bank_v, inf_v, tap_v, outf_v, bias_v,
     ask_s, asked_s, spread, red, pack, packs, tops, bots, send_cores, cores,
-    kron, moved, tapped, held, local_sem, send_sem, recv_sem,
+    kron, moved, tapped, held, local_sem, send_sem, recv_sem, hello,
 ):
     lat, lon = lax.axis_index("lat"), lax.axis_index("lon")
     up, down = lax.rem(lat + (n_lat - 1), n_lat), lax.rem(lat + 1, n_lat)
@@ -35,11 +36,28 @@
     rank = inf_v.shape[0]
     taps_rank = tap_v.shape[0]
     bank_rows = bank_v.shape[0]
-    around = [(lat, prev), (lat, nxt), (up, lon), (down, lon), (up, prev), (up, nxt), (down, prev), (down, nxt)]
-
+    z = lax.rem(lon, WAVE)
+    head, tail, odd = z == 0, z == WAVE - 1, lax.rem(lat, 2) == 1
+    even_lat = lax.rem(lat, 2) == 0
     barrier = pltpu.get_barrier_semaphore()
-    for place in around:
-        pl.semaphore_signal(barrier, inc=1, device_id=place, device_id_type=MESH)
+
+    def signal(semaphore, place):
+        pl.semaphore_signal(semaphore, inc=1, device_id=place, device_id_type=MESH)
+
+    @pl.when(z != WAVE - 1)
+    def _():
+        for line in (lat, up, down):
+            signal(barrier, (line, nxt))
+
+    @pl.when(head)
+    def _():
+        for line in (lat, up, down):
+            signal(barrier, (line, prev))
+
+    @pl.when(odd)
+    def _():
+        for line in (up, down):
+            signal(barrier, (line, lon))
 
     def local(source, target, index):
         copy = pltpu.make_async_copy(source, target, local_sem.at[index])
@@ -65,6 +83,33 @@
             device_id=place, device_id_type=MESH,
         )
 
+    count = jnp.where(head, 0, 3) + jnp.where(tail, 3, 0) + jnp.where(odd, 0, 2)
+
+    @pl.when(count > 0)
+    def _():
+        pl.semaphore_wait(barrier, count)
+
+    @pl.when(z != 0)
+    def _():
+        signal(hello.at[1], (lat, prev))
+        signal(hello.at[7], (up, prev))
+        signal(hello.at[5], (down, prev))
+
+    @pl.when(tail)
+    def _():
+        signal(hello.at[0], (lat, nxt))
+        signal(hello.at[6], (up, nxt))
+        signal(hello.at[4], (down, nxt))
+
+    @pl.when(even_lat)
+    def _():
+        signal(hello.at[3], (up, lon))
+        signal(hello.at[2], (down, lon))
+
+    def heard(*indices):
+        for index in indices:
+            pl.semaphore_wait(hello.at[index], 1)
+
     get_tr.wait()
     get_slot.wait()
     slots = [slot_s[tr_s[0, 0, j]] for j in range(MAXR)]
@@ -88,10 +133,17 @@
     ask_s[0, 0], ask_s[0, 1] = prev_a, prev_b
     ask_s[1, 0], ask_s[1, 1] = next_a, next_b
 
-    pl.semaphore_wait(barrier, len(around))
     ask_prev = remote(ask_s.at[0], asked_s.at[1], 0, (lat, prev))
     ask_next = remote(ask_s.at[1], asked_s.at[0], 1, (lat, nxt))
-    ask_prev.start()
+
+    @pl.when(z != 0)
+    def _():
+        ask_prev.start()
+
+    @pl.when(z != WAVE - 1)
+    def _():
+        heard(1)
+
     ask_next.start()
 
     get_feat.wait()
@@ -110,31 +162,60 @@
 
     edge = REACH * LANES
     whole = rows * LANES
-    rims = [
+    rims_prev = [
         remote(pack, packs.at[1], 2, (lat, prev)),
+        remote(pack, packs.at[5], 6, (up, prev)),
+        remote(pack, packs.at[3], 8, (down, prev)),
+    ]
+    rims_next = [
         remote(pack, packs.at[0], 3, (lat, nxt)),
+        remote(pack, packs.at[4], 7, (up, nxt)),
+        remote(pack, packs.at[2], 9, (down, nxt)),
+    ]
+    rims_lat = [
         remote(red.at[:, pl.ds(0, edge)], bots, 4, (up, lon)),
         remote(red.at[:, pl.ds(whole - edge, edge)], tops, 5, (down, lon)),
-        remote(pack, packs.at[5], 6, (up, prev)),
-        remote(pack, packs.at[4], 7, (up, nxt)),
-        remote(pack, packs.at[3], 8, (down, prev)),
-        remote(pack, packs.at[2], 9, (down, nxt)),
     ]
-    for copy in rims:
+    rims = rims_prev + rims_next + rims_lat
+
+    @pl.when(z != WAVE - 1)
+    def _():
+        heard(5, 7)
+
+    for copy in rims_next:
         copy.start()
+
+    @pl.when(z != 0)
+    def _():
+        for copy in rims_prev:
+            copy.start()
+
+    @pl.when(odd)
+    def _():
+        heard(2, 3)
+
+    for copy in rims_lat:
+        copy.start()
+
+    give_next = remote(send_cores.at[pl.ds(0, 2)], cores.at[pl.ds(0, 2)], 10, (lat, nxt))
+    give_prev = remote(send_cores.at[pl.ds(2, 2)], cores.at[pl.ds(2, 2)], 11, (lat, prev))
+
+    def serve_next():
+        ask_prev.wait_recv()
+        send_cores[0] = bank_v[asked_s[1, 0]]
+        send_cores[1] = bank_v[asked_s[1, 1]]
+        give_next.start()
+
+    def serve_prev():
+        ask_next.wait_recv()
+        send_cores[2] = bank_v[asked_s[0, 0]]
+        send_cores[3] = bank_v[asked_s[0, 1]]
+        give_prev.start()
 
     for copy in get_bank:
         copy.wait()
-    ask_prev.wait_recv()
-    send_cores[0] = bank_v[asked_s[1, 0]]
-    send_cores[1] = bank_v[asked_s[1, 1]]
-    ask_next.wait_recv()
-    send_cores[2] = bank_v[asked_s[0, 0]]
-    send_cores[3] = bank_v[asked_s[0, 1]]
-    give_next = remote(send_cores.at[pl.ds(0, 2)], cores.at[pl.ds(0, 2)], 10, (lat, nxt))
-    give_prev = remote(send_cores.at[pl.ds(2, 2)], cores.at[pl.ds(2, 2)], 11, (lat, prev))
-    give_next.start()
-    give_prev.start()
+    serve_next()
+    pl.when(z != 0)(serve_prev)
 
     get_tap.wait()
     depth = kron.shape[1]
@@ -149,6 +230,15 @@
             same, jnp.broadcast_to(wide[c : c + 1, :], (rank, depth)), 0.0
         ).astype(BF16)
 
+    @pl.when(head)
+    def _():
+        heard(0)
+        ask_prev.start()
+        heard(4, 6)
+        for copy in rims_prev:
+            copy.start()
+        serve_prev()
+
     for copy in rims:
         copy.wait_recv()
     not_first = (lat > 0).astype(F32)
@@ -214,7 +304,7 @@
         hidden = held[:, pl.ds(start, span)]
         for k, at in enumerate((prev_at_a, prev_at_b, next_at_a, next_at_b)):
             hidden = jnp.where(label == at, theirs[k * rank : (k + 1) * rank], hidden)
-        value = dot(last, hidden.astype(BF16)) + bias
+        value = lax.dot_general(last, hidden.astype(BF16), (((0,), (0,)), ((), ())), preferred_element_type=F32) + bias
         value = value / (1.0 + jnp.exp(-value))
         for k in range(2):
             spread[pl.ds(2 * i + k, channels, stride=rows), :] = value[:, k * LANES : (k + 1) * LANES]
@@ -242,7 +332,7 @@
     anywhere = pl.BlockSpec(memory_space=pltpu.HBM)
     return pl.pallas_call(
         functools.partial(kernel, n_lat, n_lon),
-        out_shape=jax.ShapeDtypeStruct(features.shape, BF16),
+        out_shape=pltpu.VMEM(features.shape, BF16),
         in_specs=[anywhere] * 9,
         out_specs=pl.BlockSpec(memory_space=pltpu.VMEM),
         scratch_shapes=[
@@ -253,7 +343,7 @@
             pltpu.VMEM(kernel_bank.shape, BF16),
             pltpu.VMEM(in_factor.shape, BF16),
             pltpu.VMEM(tap_factor.shape, BF16),
-            pltpu.VMEM(out_factor.shape, BF16),
+            pltpu.VMEM(out_factor.shape[::-1], BF16),
             pltpu.VMEM((1, out_bias.shape[0]), F32),
             pltpu.SMEM((2, 2), jnp.int32),
             pltpu.SMEM((2, 2), jnp.int32),
@@ -272,13 +362,14 @@
             dma((12,)),
             dma((12,)),
             dma((12,)),
+            pltpu.SemaphoreType.REGULAR((8,)),
         ],
         compiler_params=pltpu.CompilerParams(
-            collective_id=0, has_side_effects=True, vmem_limit_bytes=48 * 1024 * 1024
+            collective_id=0, has_side_effects=True, vmem_limit_bytes=56 * 1024 * 1024
         ),
         name="layer",
     )(
-        features, labels, tile_regions, bank_slot, kernel_bank, in_factor, tap_factor, out_factor,
+        features, labels, tile_regions, bank_slot, kernel_bank, in_factor, tap_factor, out_factor.T,
         out_bias.reshape(1, -1),
     )
 

time: 40.1 us -> 32.1 us (0.80)
  local copies, waits for them, and re-layouts: 8.6 us -> 0.71 us
    unnamed x18 -> x1, local copies, waits for them, and re-layouts: 8.6 us -> 0.71 us
where the time goes in v2:
time: 32.1 us; the launch traced here: 31.9 us
  Pallas kernels  31.2 us (97%)
  local copies, waits for them, and re-layouts  0.71 us (2%)
    pallas_call x1, Pallas kernels, on_device(): pl.pallas_call(functools.partial(kernel, n_lat, n_lon), out_shape=pltpu.V...  31.2 us
    unnamed x1, local copies, waits for them, and re-layouts  0.71 us

profile of v2, /device:TPU:1, one launch (start us, length us, event | category | flops | bytes accessed | tf_op | source)
XLA Modules:
  0.0 31.9 jit_solution(14924194488176434153)
XLA Ops:
  0.0 31.2 %layer.1 = bf16[64,16,128]{2,1,0:T(8,128)(2,1)S(1)} custom-call(bf16[64,16,128]{2,1,0:T(8,128)(2,1)} %feat_h.1, s32[16,128]{1,0:T(8,128)} %lab_h.1, s32[1,1,6]{2,1,0:T(1,128)} %tr_h.1, s32[5376]{0:T(1024)} %slot_h.1, bf16[112,32,512]{2,1,0:T(8,128)(2,1)} %bank_h.1, bf16[32,64]{1,0:T(8,128)(2,1)} %inf_h.1, bf16[16,25]{1,0:T(8,128)(2,1)} %tap_h.1, ...), custom_call_target="tpu_custom_call" | custom-call | tf_op jit(solution)/shard_map/layer/pallas_call | solution.py:333
  31.2 0.7 %copy.11 = bf16[64,16,128]{2,1,0:T(8,128)(2,1)} copy(bf16[64,16,128]{2,1,0:T(8,128)(2,1)S(1)} %layer.1) | data formatting | bytes 524288

commit v3 on v2

--- a/solution.py
+++ b/solution.py
@@ -27,7 +27,7 @@
     out_ref,
     feat_v, lab_v, tr_s, slot_s, bank_v, inf_v, tap_v, outf_v, bias_v,
     ask_s, asked_s, spread, red, pack, packs, tops, bots, send_cores, cores,
-    kron, moved, tapped, held, local_sem, send_sem, recv_sem, hello,
+    kron, moved, rim_cells, tapped, held, local_sem, send_sem, recv_sem, hello,
 ):
     lat, lon = lax.axis_index("lat"), lax.axis_index("lon")
     up, down = lax.rem(lat + (n_lat - 1), n_lat), lax.rem(lat + 1, n_lat)
@@ -68,14 +68,14 @@
     get_slot = local(slot_h, slot_s, 1)
     get_feat = local(feat_h, feat_v, 2)
     get_inf = local(inf_h, inf_v, 3)
+    part = bank_rows // 4
+    get_bank = [
+        local(bank_h.at[pl.ds(i * part, part)], bank_v.at[pl.ds(i * part, part)], 8 + i) for i in range(4)
+    ]
     get_tap = local(tap_h, tap_v, 4)
     get_lab = local(lab_h, lab_v, 5)
     get_outf = local(outf_h, outf_v, 6)
     get_bias = local(bias_h, bias_v, 7)
-    part = bank_rows // 4
-    get_bank = [
-        local(bank_h.at[pl.ds(i * part, part)], bank_v.at[pl.ds(i * part, part)], 8 + i) for i in range(4)
-    ]
 
     def remote(source, target, index, place):
         return pltpu.make_async_remote_copy(
@@ -127,7 +127,7 @@
             count = count + hit.astype(jnp.int32)
         return row_a, row_b, at_a, at_b
 
-    own_a, own_b, own_at, _ = wanted(lon)
+    own_a, own_b, own_at, own_at_b = wanted(lon)
     prev_a, prev_b, prev_at_a, prev_at_b = wanted(prev)
     next_a, next_b, next_at_a, next_at_b = wanted(nxt)
     ask_s[0, 0], ask_s[0, 1] = prev_a, prev_b
@@ -140,11 +140,9 @@
     def _():
         ask_prev.start()
 
-    @pl.when(z != WAVE - 1)
-    def _():
-        heard(1)
-
-    ask_next.start()
+    @pl.when(tail)
+    def _():
+        ask_next.start()
 
     get_feat.wait()
     get_inf.wait()
@@ -152,12 +150,17 @@
     lane = lax.broadcasted_iota(jnp.int32, (rank, LANES), 1)
     packed = jnp.zeros((rank, LANES), F32)
     weights = inf_v[...]
-    for r in range(rows):
-        columns = spread[pl.ds(r, channels, stride=rows), :].astype(BF16)
-        block = dot(weights, columns).astype(BF16)
-        red[:, r * LANES : (r + 1) * LANES] = block
-        rolled = pltpu.roll(block.astype(F32), (4 * r + 2) % LANES, 1)
-        packed = jnp.where((lane >= 4 * r) & (lane < 4 * r + 4), rolled, packed)
+    for r in range(0, rows, 2):
+        columns = jnp.concatenate(
+            [spread[pl.ds(r + k, channels, stride=rows), :] for k in range(2)], axis=1
+        ).astype(BF16)
+        pair = dot(weights, columns).astype(BF16)
+        red[:, r * LANES : (r + 2) * LANES] = pair
+        pair = pair.astype(F32)
+        for k in range(2):
+            at = 4 * (r + k + REACH)
+            rolled = pltpu.roll(pair[:, k * LANES : (k + 1) * LANES], (at + 2) % LANES, 1)
+            packed = jnp.where((lane >= at) & (lane < at + 4), rolled, packed)
     pack[...] = packed.astype(BF16)
 
     edge = REACH * LANES
@@ -178,17 +181,19 @@
     ]
     rims = rims_prev + rims_next + rims_lat
 
+    @pl.when(z != 0)
+    def _():
+        for copy in rims_prev:
+            copy.start()
+
     @pl.when(z != WAVE - 1)
     def _():
+        heard(1)
+        ask_next.start()
         heard(5, 7)
 
     for copy in rims_next:
         copy.start()
-
-    @pl.when(z != 0)
-    def _():
-        for copy in rims_prev:
-            copy.start()
 
     @pl.when(odd)
     def _():
@@ -230,6 +235,75 @@
             same, jnp.broadcast_to(wide[c : c + 1, :], (rank, depth)), 0.0
         ).astype(BF16)
 
+    not_first = (lat > 0).astype(F32)
+    not_last = (lat < n_lat - 1).astype(F32)
+
+    def place_row(at, block):
+        here = (lane >= 4 * at) & (lane < 4 * at + 4)
+        for dx in range(KS):
+            rolled = block if dx == REACH else pltpu.roll(block, (REACH - dx) % LANES, 1)
+            moved[dx * rank : (dx + 1) * rank, at * LANES : (at + 1) * LANES] = rolled.astype(BF16)
+            ends = pltpu.roll(block, (4 * at + 4 - dx) % LANES, 1)
+            rim_cells[dx] = jnp.where(here, ends, rim_cells[dx])
+
+    for dx in range(KS):
+        rim_cells[dx] = jnp.zeros((rank, LANES), F32)
+    for r in range(rows):
+        place_row(REACH + r, red[:, r * LANES : (r + 1) * LANES].astype(F32))
+
+    get_lab.wait()
+    own_cores = jnp.concatenate([bank_v[own_a], bank_v[own_b]], axis=0)
+    span = 2 * LANES
+    blank = jnp.zeros((depth - KS * KS * rank, span), BF16)
+
+    def label_row(r):
+        return jnp.broadcast_to(lab_v[pl.ds(r, 1), :], (rank, LANES))
+
+    def label_pair(i):
+        return jnp.concatenate([label_row(2 * i), label_row(2 * i + 1)], axis=1)
+
+    def tap_rows(i):
+        start = pl.multiple_of(i * span, span)
+        pieces = [moved[:, pl.ds(pl.multiple_of(start + dy * LANES, LANES), span)] for dy in range(KS)]
+        result = dot(kron[...], jnp.concatenate(pieces + [blank], axis=0)).astype(BF16)
+        tapped[:, pl.ds(start, span)] = result
+        ours = dot(own_cores, result)
+        held[:, pl.ds(start, span)] = jnp.where(label_pair(i) == own_at, ours[:rank], ours[rank:])
+
+    pl.loop(1, rows // 2 - 1)(tap_rows)
+    for copy in rims_lat:
+        copy.wait_recv()
+    for r in range(REACH):
+        lanes = pl.ds(r * LANES, LANES)
+        place_row(r, tops[:, lanes].astype(F32) * not_first)
+        place_row(rows + REACH + r, bots[:, lanes].astype(F32) * not_last)
+    pl.loop(0, 2)(lambda k: tap_rows(k * (rows // 2 - 1)))
+
+    give_prev.wait_recv()
+    next_cores = cores[pl.ds(2, 2)].reshape(2 * rank, cores.shape[2])
+
+    @pl.loop(0, rows // 4, unroll=2)
+    def _(i):
+        start = pl.multiple_of(i * 2 * span, 2 * span)
+        theirs = dot(next_cores, tapped[:, pl.ds(start, 2 * span)])
+        label = jnp.concatenate([label_pair(2 * i), label_pair(2 * i + 1)], axis=1)
+        hidden = held[:, pl.ds(start, 2 * span)]
+        hidden = jnp.where(label == next_at_a, theirs[:rank], hidden)
+        held[:, pl.ds(start, 2 * span)] = jnp.where(label == next_at_b, theirs[rank:], hidden)
+
+    get_outf.wait()
+    get_bias.wait()
+    square = (channels, channels)
+    eye = lax.broadcasted_iota(jnp.int32, square, 0) == lax.broadcasted_iota(jnp.int32, square, 1)
+    bias = jnp.sum(jnp.where(eye, jnp.broadcast_to(bias_v[...], square), 0.0), axis=1, keepdims=True)
+    lab_lane = lax.broadcasted_iota(jnp.int32, (rows, LANES), 1)
+    lab_at = 4 * lax.broadcasted_iota(jnp.int32, (rows, LANES), 0)
+    lab_rolled = pltpu.roll(lab_v[...], 2, 1, stride=4, stride_axis=0)
+    rim_label = jnp.sum(
+        jnp.where((lab_lane >= lab_at) & (lab_lane < lab_at + 4), lab_rolled, 0), axis=0, keepdims=True
+    )
+    rim_label = jnp.broadcast_to(rim_label, (rank, LANES))
+
     @pl.when(head)
     def _():
         heard(0)
@@ -239,75 +313,62 @@
             copy.start()
         serve_prev()
 
-    for copy in rims:
+    for copy in rims_prev + rims_next:
         copy.wait_recv()
-    not_first = (lat > 0).astype(F32)
-    not_last = (lat < n_lat - 1).astype(F32)
     even = lane % 4 < 2
-
-    def place_row(at, block, sides, row):
-        beside = pltpu.roll(sides, (LANES - 2 - 4 * row) % LANES, 1)
-        shapes = (
-            pltpu.roll(jnp.where(lane >= LANES - 2, beside, block), 2, 1),
-            pltpu.roll(jnp.where(lane == LANES - 1, beside, block), 1, 1),
-            block,
-            pltpu.roll(jnp.where(lane == 0, beside, block), LANES - 1, 1),
-            pltpu.roll(jnp.where(lane < 2, beside, block), LANES - 2, 1),
-        )
-        for dx in range(KS):
-            moved[dx * rank : (dx + 1) * rank, at * LANES : (at + 1) * LANES] = shapes[dx].astype(BF16)
-
-    middle = jnp.where(even, packs[0].astype(F32), packs[1].astype(F32))
-    above = jnp.where(even, packs[2].astype(F32), packs[3].astype(F32)) * not_first
-    below = jnp.where(even, packs[4].astype(F32), packs[5].astype(F32)) * not_last
-    for r in range(REACH):
-        lanes = pl.ds(r * LANES, LANES)
-        place_row(r, tops[:, lanes].astype(F32) * not_first, above, rows - REACH + r)
-        place_row(rows + REACH + r, bots[:, lanes].astype(F32) * not_last, below, r)
-    for r in range(rows):
-        place_row(REACH + r, red[:, r * LANES : (r + 1) * LANES].astype(F32), middle, r)
-
-    get_lab.wait()
-    own_cores = jnp.concatenate([bank_v[own_a], bank_v[own_b]], axis=0)
-    span = 2 * LANES
-
-    def label_of(i):
-        return jnp.concatenate(
-            [jnp.broadcast_to(lab_v[pl.ds(2 * i + k, 1), :], (rank, LANES)) for k in range(2)], axis=1
-        )
-
-    @pl.loop(0, rows // 2)
-    def _(i):
-        start = pl.multiple_of(i * span, span)
-        pieces = [moved[:, pl.ds(pl.multiple_of(start + dy * LANES, LANES), span)] for dy in range(KS)]
-        pieces.append(jnp.zeros((depth - KS * KS * rank, span), BF16))
-        result = dot(kron[...], jnp.concatenate(pieces, axis=0)).astype(BF16)
-        tapped[:, pl.ds(start, span)] = result
-        ours = dot(own_cores, result)
-        held[:, pl.ds(start, span)] = jnp.where(label_of(i) == own_at, ours[:rank], ours[rank:])
-
-    get_outf.wait()
-    get_bias.wait()
-    square = (channels, channels)
-    eye = lax.broadcasted_iota(jnp.int32, square, 0) == lax.broadcasted_iota(jnp.int32, square, 1)
-    bias = jnp.sum(jnp.where(eye, jnp.broadcast_to(bias_v[...], square), 0.0), axis=1, keepdims=True)
+    middle, above, below = (
+        jnp.where(even, packs[2 * k].astype(F32), packs[2 * k + 1].astype(F32)) for k in range(3)
+    )
+    above = pltpu.roll(above, LANES // 2, 1) * not_first
+    below = pltpu.roll(below, LANES // 2, 1) * not_last
+    sides = jnp.where(lane < 4 * REACH, above, jnp.where(lane < 4 * (rows + REACH), middle, below))
+    spot = lane % 4
+    fixed = (
+        jnp.where(spot >= 2, pltpu.roll(sides, 2, 1), rim_cells[0]),
+        jnp.where(spot == 2, pltpu.roll(sides, 1, 1), rim_cells[1]),
+        rim_cells[2],
+        jnp.where(spot == 1, pltpu.roll(sides, LANES - 1, 1), rim_cells[3]),
+        jnp.where(spot < 2, pltpu.roll(sides, LANES - 2, 1), rim_cells[4]),
+    )
+    pieces = [
+        (pltpu.roll(fixed[dx], LANES - 4 * dy, 1) if dy else fixed[dx]).astype(BF16)
+        for dy in range(KS)
+        for dx in range(KS)
+    ]
+    rim_tapped = dot(kron[...], jnp.concatenate(pieces + [blank[:, :LANES]], axis=0)).astype(BF16)
+    ready = jnp.concatenate([own_cores, next_cores], axis=0)
+    theirs = dot(ready, rim_tapped)
+    rim_hidden = theirs[:rank]
+    for k, at in enumerate((own_at_b, next_at_a, next_at_b)):
+        rim_hidden = jnp.where(rim_label == at, theirs[(k + 1) * rank : (k + 2) * rank], rim_hidden)
+
     give_next.wait_recv()
-    give_prev.wait_recv()
-    others = cores[...].reshape(4 * rank, cores.shape[2])
+    prev_cores = cores[pl.ds(0, 2)].reshape(2 * rank, cores.shape[2])
     last = outf_v[...]
-
-    @pl.loop(0, rows // 2)
-    def _(i):
-        start = pl.multiple_of(i * span, span)
-        theirs = dot(others, tapped[:, pl.ds(start, span)])
-        label = label_of(i)
-        hidden = held[:, pl.ds(start, span)]
-        for k, at in enumerate((prev_at_a, prev_at_b, next_at_a, next_at_b)):
-            hidden = jnp.where(label == at, theirs[k * rank : (k + 1) * rank], hidden)
-        value = lax.dot_general(last, hidden.astype(BF16), (((0,), (0,)), ((), ())), preferred_element_type=F32) + bias
+    theirs = dot(prev_cores, rim_tapped)
+    rim_hidden = jnp.where(rim_label == prev_at_a, theirs[:rank], rim_hidden)
+    rim_hidden = jnp.where(rim_label == prev_at_b, theirs[rank:], rim_hidden)
+    at_rim = (lane < REACH) | (lane >= LANES - REACH)
+    group = 4
+    for first in range(0, rows, group):
+        width = group * LANES
+        theirs = dot(prev_cores, tapped[:, first * LANES : first * LANES + width])
+        parts = []
+        for k in range(group):
+            r = first + k
+            label = label_row(r)
+            mine = slice(k * LANES, (k + 1) * LANES)
+            hidden = held[:, r * LANES : (r + 1) * LANES]
+            hidden = jnp.where(label == prev_at_a, theirs[:rank, mine], hidden)
+            hidden = jnp.where(label == prev_at_b, theirs[rank:, mine], hidden)
+            beside = pltpu.roll(rim_hidden, (LANES - 2 - 4 * r) % LANES, 1)
+            parts.append(jnp.where(at_rim, beside, hidden).astype(BF16))
+        value = lax.dot_general(
+            last, jnp.concatenate(parts, axis=1), (((0,), (0,)), ((), ())), preferred_element_type=F32
+        ) + bias
         value = value / (1.0 + jnp.exp(-value))
-        for k in range(2):
-            spread[pl.ds(2 * i + k, channels, stride=rows), :] = value[:, k * LANES : (k + 1) * LANES]
+        for k in range(group):
+            spread[pl.ds(first + k, channels, stride=rows), :] = value[:, k * LANES : (k + 1) * LANES]
 
     out_ref[...] = spread[...].reshape(channels, rows, LANES).astype(BF16)
 
@@ -357,6 +418,7 @@
             pltpu.VMEM((4, rank, width), BF16),
             pltpu.VMEM((taps_rank * rank, depth), BF16),
             pltpu.VMEM((KS * rank, wide), BF16),
+            pltpu.VMEM((KS, rank, columns), F32),
             pltpu.VMEM((taps_rank * rank, cells), BF16),
             pltpu.VMEM((rank, cells), F32),
             dma((12,)),

time: 32.1 us -> 29.6 us (0.922)
  the two profiles are of different devices: /device:TPU:1 before, /device:TPU:8 now
where the time goes in v3:
time: 29.6 us; the launch traced here: 29.5 us
  Pallas kernels  28.8 us (97%)
  local copies, waits for them, and re-layouts  0.71 us (2%)
    pallas_call x1, Pallas kernels, on_device(): pl.pallas_call(functools.partial(kernel, n_lat, n_lon), out_shape=pltpu.V...  28.8 us
    unnamed x1, local copies, waits for them, and re-layouts  0.71 us

profile of v3, /device:TPU:8, one launch (start us, length us, event | category | flops | bytes accessed | tf_op | source)
XLA Modules:
  0.0 29.5 jit_solution(15792409943263903816)
XLA Ops:
  0.0 28.8 %layer.1 = bf16[64,16,128]{2,1,0:T(8,128)(2,1)S(1)} custom-call(bf16[64,16,128]{2,1,0:T(8,128)(2,1)} %feat_h.1, s32[16,128]{1,0:T(8,128)} %lab_h.1, s32[1,1,6]{2,1,0:T(1,128)} %tr_h.1, s32[5376]{0:T(1024)} %slot_h.1, bf16[112,32,512]{2,1,0:T(8,128)(2,1)} %bank_h.1, bf16[32,64]{1,0:T(8,128)(2,1)} %inf_h.1, bf16[16,25]{1,0:T(8,128)(2,1)} %tap_h.1, ...), custom_call_target="tpu_custom_call" | custom-call | tf_op jit(solution)/shard_map/layer/pallas_call | solution.py:394
  28.8 0.7 %copy.11 = bf16[64,16,128]{2,1,0:T(8,128)(2,1)} copy(bf16[64,16,128]{2,1,0:T(8,128)(2,1)S(1)} %layer.1) | data formatting | bytes 524288

commit v4 on v3

--- a/solution.py
+++ b/solution.py
@@ -26,7 +26,7 @@
     feat_h, lab_h, tr_h, slot_h, bank_h, inf_h, tap_h, outf_h, bias_h,
     out_ref,
     feat_v, lab_v, tr_s, slot_s, bank_v, inf_v, tap_v, outf_v, bias_v,
-    ask_s, asked_s, spread, red, pack, packs, tops, bots, send_cores, cores,
+    ask_s, asked_s, relay_s, spread, red, pack, packs, tops, bots, send_cores, cores,
     kron, moved, rim_cells, tapped, held, local_sem, send_sem, recv_sem, hello,
 ):
     lat, lon = lax.axis_index("lat"), lax.axis_index("lon")
@@ -39,6 +39,7 @@
     z = lax.rem(lon, WAVE)
     head, tail, odd = z == 0, z == WAVE - 1, lax.rem(lat, 2) == 1
     even_lat = lax.rem(lat, 2) == 0
+    odd_lat = lat + 1 - lax.rem(lat, 2)
     barrier = pltpu.get_barrier_semaphore()
 
     def signal(semaphore, place):
@@ -49,10 +50,22 @@
         for line in (lat, up, down):
             signal(barrier, (line, nxt))
 
+    round_trip = lambda steps: lax.rem(lon + steps + n_lon, n_lon)
+    head_before, head_after = round_trip(-WAVE), round_trip(WAVE)
+    my_tail, my_head = round_trip(WAVE - 1), round_trip(1 - WAVE)
+
     @pl.when(head)
     def _():
         for line in (lat, up, down):
             signal(barrier, (line, prev))
+
+    relay = head & odd
+
+    @pl.when(relay)
+    def _():
+        for line in (lat, up):
+            signal(barrier, (line, my_tail))
+            signal(barrier, (line, head_after))
 
     @pl.when(odd)
     def _():
@@ -77,29 +90,29 @@
     get_outf = local(outf_h, outf_v, 6)
     get_bias = local(bias_h, bias_v, 7)
 
-    def remote(source, target, index, place):
+    def remote(source, target, index, place, lands=None):
+        lands = index if lands is None else lands
         return pltpu.make_async_remote_copy(
-            src_ref=source, dst_ref=target, send_sem=send_sem.at[index], recv_sem=recv_sem.at[index],
+            src_ref=source, dst_ref=target, send_sem=send_sem.at[index], recv_sem=recv_sem.at[lands],
             device_id=place, device_id_type=MESH,
         )
 
-    count = jnp.where(head, 0, 3) + jnp.where(tail, 3, 0) + jnp.where(odd, 0, 2)
-
-    @pl.when(count > 0)
-    def _():
-        pl.semaphore_wait(barrier, count)
+    count = jnp.where(head, 1, 3) + jnp.where(tail, 4, 0) + jnp.where(odd, 0, 2)
+
+    pl.semaphore_wait(barrier, count)
+
+    @pl.when(tail)
+    def _():
+        signal(hello.at[8 + lax.rem(lat, 2)], (odd_lat, my_head))
+        signal(hello.at[0], (lat, nxt))
+        signal(hello.at[6], (up, nxt))
+        signal(hello.at[4], (down, nxt))
 
     @pl.when(z != 0)
     def _():
         signal(hello.at[1], (lat, prev))
         signal(hello.at[7], (up, prev))
         signal(hello.at[5], (down, prev))
-
-    @pl.when(tail)
-    def _():
-        signal(hello.at[0], (lat, nxt))
-        signal(hello.at[6], (up, nxt))
-        signal(hello.at[4], (down, nxt))
 
     @pl.when(even_lat)
     def _():
@@ -135,6 +148,13 @@
 
     ask_prev = remote(ask_s.at[0], asked_s.at[1], 0, (lat, prev))
     ask_next = remote(ask_s.at[1], asked_s.at[0], 1, (lat, nxt))
+    ask_relay = remote(
+        ask_s.at[0], relay_s.at[lax.rem(lat, 2)], 12, (odd_lat, head_before), lands=12 + lax.rem(lat, 2)
+    )
+    relayed = [remote(ask_s.at[0], relay_s.at[k], 12, (odd_lat, head_before), lands=12 + k) for k in range(2)]
+    forward = [
+        remote(relay_s.at[k], asked_s.at[1], 13 + k, (line, my_tail), lands=0) for k, line in enumerate((up, lat))
+    ]
 
     @pl.when(z != 0)
     def _():
@@ -181,27 +201,6 @@
     ]
     rims = rims_prev + rims_next + rims_lat
 
-    @pl.when(z != 0)
-    def _():
-        for copy in rims_prev:
-            copy.start()
-
-    @pl.when(z != WAVE - 1)
-    def _():
-        heard(1)
-        ask_next.start()
-        heard(5, 7)
-
-    for copy in rims_next:
-        copy.start()
-
-    @pl.when(odd)
-    def _():
-        heard(2, 3)
-
-    for copy in rims_lat:
-        copy.start()
-
     give_next = remote(send_cores.at[pl.ds(0, 2)], cores.at[pl.ds(0, 2)], 10, (lat, nxt))
     give_prev = remote(send_cores.at[pl.ds(2, 2)], cores.at[pl.ds(2, 2)], 11, (lat, prev))
 
@@ -217,10 +216,39 @@
         send_cores[3] = bank_v[asked_s[0, 1]]
         give_prev.start()
 
+    def send(copies):
+        for copy in copies:
+            copy.start()
+
+    @pl.when(tail)
+    def _():
+        send(rims_next)
+
+    @pl.when(z != 0)
+    def _():
+        send(rims_prev)
+
     for copy in get_bank:
         copy.wait()
-    serve_next()
+    pl.when(tail)(serve_next)
+
+    def send_lat():
+        pl.when(odd)(lambda: heard(2, 3))
+        send(rims_lat)
+
+    pl.when(z != 0)(send_lat)
+
+    @pl.when(z != WAVE - 1)
+    def _():
+        heard(1)
+        ask_next.start()
+        heard(5, 7)
+        send(rims_next)
+        serve_next()
+
     pl.when(z != 0)(serve_prev)
+
+    pl.when(head)(ask_relay.start)
 
     get_tap.wait()
     depth = kron.shape[1]
@@ -271,6 +299,20 @@
         held[:, pl.ds(start, span)] = jnp.where(label_pair(i) == own_at, ours[:rank], ours[rank:])
 
     pl.loop(1, rows // 2 - 1)(tap_rows)
+    pl.when(head)(send_lat)
+
+    @pl.when(relay)
+    def _():
+        for k in (1, 0):
+            relayed[k].wait_recv()
+            heard(8 + k)
+            forward[k].start()
+
+    @pl.when(head)
+    def _():
+        heard(0, 4, 6)
+        send(rims_prev)
+
     for copy in rims_lat:
         copy.wait_recv()
     for r in range(REACH):
@@ -304,14 +346,7 @@
     )
     rim_label = jnp.broadcast_to(rim_label, (rank, LANES))
 
-    @pl.when(head)
-    def _():
-        heard(0)
-        ask_prev.start()
-        heard(4, 6)
-        for copy in rims_prev:
-            copy.start()
-        serve_prev()
+    pl.when(head)(serve_prev)
 
     for copy in rims_prev + rims_next:
         copy.wait_recv()
@@ -372,7 +407,17 @@
 
     out_ref[...] = spread[...].reshape(channels, rows, LANES).astype(BF16)
 
-    ask_prev.wait_send()
+    pl.when(head)(ask_relay.wait_send)
+
+    @pl.when(relay)
+    def _():
+        for copy in forward:
+            copy.wait_send()
+
+    @pl.when(z != 0)
+    def _():
+        ask_prev.wait_send()
+
     ask_next.wait_send()
     for copy in rims:
         copy.wait_send()
@@ -408,6 +453,7 @@
             pltpu.VMEM((1, out_bias.shape[0]), F32),
             pltpu.SMEM((2, 2), jnp.int32),
             pltpu.SMEM((2, 2), jnp.int32),
+            pltpu.SMEM((2, 2), jnp.int32),
             pltpu.VMEM((channels * rows, columns), F32),
             pltpu.VMEM((rank, cells), BF16),
             pltpu.VMEM((rank, columns), BF16),
@@ -422,9 +468,9 @@
             pltpu.VMEM((taps_rank * rank, cells), BF16),
             pltpu.VMEM((rank, cells), F32),
             dma((12,)),
-            dma((12,)),
-            dma((12,)),
-            pltpu.SemaphoreType.REGULAR((8,)),
+            dma((15,)),
+            dma((14,)),
+            pltpu.SemaphoreType.REGULAR((10,)),
         ],
         compiler_params=pltpu.CompilerParams(
             collective_id=0, has_side_effects=True, vmem_limit_bytes=56 * 1024 * 1024

time: 29.6 us -> 27.1 us (0.916)
  the two profiles are of different devices: /device:TPU:8 before, /device:TPU:24 now
where the time goes in v4:
time: 27.1 us; the launch traced here: 27 us
  Pallas kernels  26.3 us (97%)
  local copies, waits for them, and re-layouts  0.71 us (3%)
    pallas_call x1, Pallas kernels, on_device(): pl.pallas_call(functools.partial(kernel, n_lat, n_lon), out_shape=pltpu.V...  26.3 us
    unnamed x1, local copies, waits for them, and re-layouts  0.71 us

profile of v4, /device:TPU:24, one launch (start us, length us, event | category | flops | bytes accessed | tf_op | source)
XLA Modules:
  0.0 27.0 jit_solution(3312271281848496807)
XLA Ops:
  0.0 26.3 %layer.1 = bf16[64,16,128]{2,1,0:T(8,128)(2,1)S(1)} custom-call(bf16[64,16,128]{2,1,0:T(8,128)(2,1)} %feat_h.1, s32[16,128]{1,0:T(8,128)} %lab_h.1, s32[1,1,6]{2,1,0:T(1,128)} %tr_h.1, s32[5376]{0:T(1024)} %slot_h.1, bf16[112,32,512]{2,1,0:T(8,128)(2,1)} %bank_h.1, bf16[32,64]{1,0:T(8,128)(2,1)} %inf_h.1, bf16[16,25]{1,0:T(8,128)(2,1)} %tap_h.1, ...), custom_call_target="tpu_custom_call" | custom-call | tf_op jit(solution)/shard_map/layer/pallas_call | solution.py:439
  26.3 0.7 %copy.11 = bf16[64,16,128]{2,1,0:T(8,128)(2,1)} copy(bf16[64,16,128]{2,1,0:T(8,128)(2,1)S(1)} %layer.1) | data formatting | bytes 524288

commit v5 on v4

--- a/solution.py
+++ b/solution.py
@@ -45,10 +45,15 @@
     def signal(semaphore, place):
         pl.semaphore_signal(semaphore, inc=1, device_id=place, device_id_type=MESH)
 
-    @pl.when(z != WAVE - 1)
+    @pl.when(z < WAVE - 2)
     def _():
         for line in (lat, up, down):
             signal(barrier, (line, nxt))
+
+    @pl.when(tail)
+    def _():
+        for line in (lat, up, down):
+            signal(barrier, (line, prev))
 
     round_trip = lambda steps: lax.rem(lon + steps + n_lon, n_lon)
     head_before, head_after = round_trip(-WAVE), round_trip(WAVE)
@@ -67,10 +72,18 @@
             signal(barrier, (line, my_tail))
             signal(barrier, (line, head_after))
 
-    @pl.when(odd)
+    @pl.when(odd & (z != WAVE - 1))
     def _():
         for line in (up, down):
             signal(barrier, (line, lon))
+
+    @pl.when(tail)
+    def _():
+        pl.semaphore_wait(barrier, 4)
+        signal(hello.at[8 + lax.rem(lat, 2)], (odd_lat, my_head))
+        signal(hello.at[0], (lat, nxt))
+        signal(hello.at[6], (up, nxt))
+        signal(hello.at[4], (down, nxt))
 
     def local(source, target, index):
         copy = pltpu.make_async_copy(source, target, local_sem.at[index])
@@ -97,27 +110,27 @@
             device_id=place, device_id_type=MESH,
         )
 
-    count = jnp.where(head, 1, 3) + jnp.where(tail, 4, 0) + jnp.where(odd, 0, 2)
-
-    pl.semaphore_wait(barrier, count)
-
-    @pl.when(tail)
-    def _():
-        signal(hello.at[8 + lax.rem(lat, 2)], (odd_lat, my_head))
+    @pl.when(z != WAVE - 1)
+    def _():
+        before = jnp.where(head, 1, 3) + jnp.where(z == WAVE - 2, 3, 0)
+        pl.semaphore_wait(barrier, before + jnp.where(odd, 0, 2))
+
+        @pl.when(even_lat)
+        def _():
+            signal(hello.at[3], (up, lon))
+            signal(hello.at[2], (down, lon))
+
+    @pl.when((z != 0) & (z != WAVE - 1))
+    def _():
+        signal(hello.at[1], (lat, prev))
+        signal(hello.at[7], (up, prev))
+        signal(hello.at[5], (down, prev))
+
+    @pl.when(z == WAVE - 2)
+    def _():
         signal(hello.at[0], (lat, nxt))
         signal(hello.at[6], (up, nxt))
         signal(hello.at[4], (down, nxt))
-
-    @pl.when(z != 0)
-    def _():
-        signal(hello.at[1], (lat, prev))
-        signal(hello.at[7], (up, prev))
-        signal(hello.at[5], (down, prev))
-
-    @pl.when(even_lat)
-    def _():
-        signal(hello.at[3], (up, lon))
-        signal(hello.at[2], (down, lon))
 
     def heard(*indices):
         for index in indices:
@@ -156,7 +169,7 @@
         remote(relay_s.at[k], asked_s.at[1], 13 + k, (line, my_tail), lands=0) for k, line in enumerate((up, lat))
     ]
 
-    @pl.when(z != 0)
+    @pl.when((z != 0) & (z != WAVE - 1))
     def _():
         ask_prev.start()
 
@@ -224,25 +237,32 @@
     def _():
         send(rims_next)
 
-    @pl.when(z != 0)
+    @pl.when((z != 0) & (z != WAVE - 1))
     def _():
         send(rims_prev)
 
     for copy in get_bank:
         copy.wait()
-    pl.when(tail)(serve_next)
+
+    @pl.when(tail)
+    def _():
+        serve_next()
+        heard(0)
+        ask_prev.start()
+        heard(4, 6)
+        send(rims_prev)
 
     def send_lat():
-        pl.when(odd)(lambda: heard(2, 3))
+        pl.when(odd & (z != WAVE - 1))(lambda: heard(2, 3))
         send(rims_lat)
 
-    pl.when(z != 0)(send_lat)
+    pl.when((z != 0) | even_lat)(send_lat)
 
     @pl.when(z != WAVE - 1)
     def _():
-        heard(1)
+        pl.when(z != WAVE - 2)(lambda: heard(1))
         ask_next.start()
-        heard(5, 7)
+        pl.when(z != WAVE - 2)(lambda: heard(5, 7))
         send(rims_next)
         serve_next()
 
@@ -299,7 +319,7 @@
         held[:, pl.ds(start, span)] = jnp.where(label_pair(i) == own_at, ours[:rank], ours[rank:])
 
     pl.loop(1, rows // 2 - 1)(tap_rows)
-    pl.when(head)(send_lat)
+    pl.when(relay)(send_lat)
 
     @pl.when(relay)
     def _():

time: 27.1 us -> 25.3 us (0.934)
  the two profiles are of different devices: /device:TPU:24 before, /device:TPU:2 now
where the time goes in v5:
time: 25.3 us; the launch traced here: 25.2 us
  Pallas kernels  24.5 us (97%)
  local copies, waits for them, and re-layouts  0.71 us (3%)
    pallas_call x1, Pallas kernels, on_device(): pl.pallas_call(functools.partial(kernel, n_lat, n_lon), out_shape=pltpu.V...  24.5 us
    unnamed x1, local copies, waits for them, and re-layouts  0.71 us

profile of v5, /device:TPU:2, one launch (start us, length us, event | category | flops | bytes accessed | tf_op | source)
XLA Modules:
  0.0 25.2 jit_solution(6769723841911805982)
XLA Ops:
  0.0 24.5 %layer.1 = bf16[64,16,128]{2,1,0:T(8,128)(2,1)S(1)} custom-call(bf16[64,16,128]{2,1,0:T(8,128)(2,1)} %feat_h.1, s32[16,128]{1,0:T(8,128)} %lab_h.1, s32[1,1,6]{2,1,0:T(1,128)} %tr_h.1, s32[5376]{0:T(1024)} %slot_h.1, bf16[112,32,512]{2,1,0:T(8,128)(2,1)} %bank_h.1, bf16[32,64]{1,0:T(8,128)(2,1)} %inf_h.1, bf16[16,25]{1,0:T(8,128)(2,1)} %tap_h.1, ...), custom_call_target="tpu_custom_call" | custom-call | tf_op jit(solution)/shard_map/layer/pallas_call | solution.py:459
  24.5 0.7 %copy.11 = bf16[64,16,128]{2,1,0:T(8,128)(2,1)} copy(bf16[64,16,128]{2,1,0:T(8,128)(2,1)S(1)} %layer.1) | data formatting | bytes 524288

commit v6 on v5

--- a/solution.py
+++ b/solution.py
@@ -26,7 +26,7 @@
     feat_h, lab_h, tr_h, slot_h, bank_h, inf_h, tap_h, outf_h, bias_h,
     out_ref,
     feat_v, lab_v, tr_s, slot_s, bank_v, inf_v, tap_v, outf_v, bias_v,
-    ask_s, asked_s, relay_s, spread, red, pack, packs, tops, bots, send_cores, cores,
+    ask_s, asked_s, relay_s, relayed_s, spread, red, pack, packs, tops, bots, send_cores, cores,
     kron, moved, rim_cells, tapped, held, local_sem, send_sem, recv_sem, hello,
 ):
     lat, lon = lax.axis_index("lat"), lax.axis_index("lon")
@@ -45,12 +45,14 @@
     def signal(semaphore, place):
         pl.semaphore_signal(semaphore, inc=1, device_id=place, device_id_type=MESH)
 
-    @pl.when(z < WAVE - 2)
+    second, middle = z == 1, (z >= 2) & (z <= WAVE - 2)
+
+    @pl.when((z >= 1) & (z < WAVE - 2))
     def _():
         for line in (lat, up, down):
             signal(barrier, (line, nxt))
 
-    @pl.when(tail)
+    @pl.when(tail | second)
     def _():
         for line in (lat, up, down):
             signal(barrier, (line, prev))
@@ -68,8 +70,8 @@
 
     @pl.when(relay)
     def _():
+        signal(barrier, (lat, my_tail))
         for line in (lat, up):
-            signal(barrier, (line, my_tail))
             signal(barrier, (line, head_after))
 
     @pl.when(odd & (z != WAVE - 1))
@@ -79,8 +81,8 @@
 
     @pl.when(tail)
     def _():
-        pl.semaphore_wait(barrier, 4)
-        signal(hello.at[8 + lax.rem(lat, 2)], (odd_lat, my_head))
+        pl.semaphore_wait(barrier, jnp.where(odd, 4, 3))
+        pl.when(odd)(lambda: signal(hello.at[8], (lat, my_head)))
         signal(hello.at[0], (lat, nxt))
         signal(hello.at[6], (up, nxt))
         signal(hello.at[4], (down, nxt))
@@ -110,23 +112,24 @@
             device_id=place, device_id_type=MESH,
         )
 
-    @pl.when(z != WAVE - 1)
-    def _():
-        before = jnp.where(head, 1, 3) + jnp.where(z == WAVE - 2, 3, 0)
-        pl.semaphore_wait(barrier, before + jnp.where(odd, 0, 2))
-
-        @pl.when(even_lat)
-        def _():
-            signal(hello.at[3], (up, lon))
-            signal(hello.at[2], (down, lon))
-
-    @pl.when((z != 0) & (z != WAVE - 1))
+    count = jnp.where(head, 4, jnp.where(second, 0, 3)) + jnp.where(z == WAVE - 2, 3, 0) + jnp.where(odd, 0, 2)
+
+    @pl.when((z != WAVE - 1) & (count > 0))
+    def _():
+        pl.semaphore_wait(barrier, count)
+
+    @pl.when(even_lat & (z != WAVE - 1))
+    def _():
+        signal(hello.at[3], (up, lon))
+        signal(hello.at[2], (down, lon))
+
+    @pl.when(middle)
     def _():
         signal(hello.at[1], (lat, prev))
         signal(hello.at[7], (up, prev))
         signal(hello.at[5], (down, prev))
 
-    @pl.when(z == WAVE - 2)
+    @pl.when(head | (z == WAVE - 2))
     def _():
         signal(hello.at[0], (lat, nxt))
         signal(hello.at[6], (up, nxt))
@@ -165,13 +168,15 @@
         ask_s.at[0], relay_s.at[lax.rem(lat, 2)], 12, (odd_lat, head_before), lands=12 + lax.rem(lat, 2)
     )
     relayed = [remote(ask_s.at[0], relay_s.at[k], 12, (odd_lat, head_before), lands=12 + k) for k in range(2)]
-    forward = [
-        remote(relay_s.at[k], asked_s.at[1], 13 + k, (line, my_tail), lands=0) for k, line in enumerate((up, lat))
-    ]
-
-    @pl.when((z != 0) & (z != WAVE - 1))
-    def _():
-        ask_prev.start()
+    forward = remote(relay_s, relayed_s, 13, (lat, my_tail), lands=14)
+
+    pl.when(middle)(ask_prev.start)
+
+    @pl.when(head)
+    def _():
+        ask_relay.start()
+        ask_next.start()
+
 
     @pl.when(tail)
     def _():
@@ -223,6 +228,17 @@
         send_cores[1] = bank_v[asked_s[1, 1]]
         give_next.start()
 
+    give_pair = remote(send_cores.at[pl.ds(4, 2)], cores.at[pl.ds(0, 2)], 14, (up, nxt), lands=10)
+
+    def serve_heads():
+        forward.wait_recv()
+        send_cores[0] = bank_v[relayed_s[1, 0]]
+        send_cores[1] = bank_v[relayed_s[1, 1]]
+        give_next.start()
+        send_cores[4] = bank_v[relayed_s[0, 0]]
+        send_cores[5] = bank_v[relayed_s[0, 1]]
+        give_pair.start()
+
     def serve_prev():
         ask_next.wait_recv()
         send_cores[2] = bank_v[asked_s[0, 0]]
@@ -233,32 +249,35 @@
         for copy in copies:
             copy.start()
 
-    @pl.when(tail)
+    @pl.when(head | tail)
     def _():
         send(rims_next)
 
-    @pl.when((z != 0) & (z != WAVE - 1))
+    @pl.when(middle)
     def _():
         send(rims_prev)
 
     for copy in get_bank:
         copy.wait()
 
-    @pl.when(tail)
-    def _():
-        serve_next()
+    def greet_prev():
         heard(0)
         ask_prev.start()
         heard(4, 6)
         send(rims_prev)
 
+    @pl.when(tail)
+    def _():
+        pl.when(odd)(serve_heads)
+        greet_prev()
+
     def send_lat():
         pl.when(odd & (z != WAVE - 1))(lambda: heard(2, 3))
         send(rims_lat)
 
     pl.when((z != 0) | even_lat)(send_lat)
 
-    @pl.when(z != WAVE - 1)
+    @pl.when(second | middle)
     def _():
         pl.when(z != WAVE - 2)(lambda: heard(1))
         ask_next.start()
@@ -266,9 +285,7 @@
         send(rims_next)
         serve_next()
 
-    pl.when(z != 0)(serve_prev)
-
-    pl.when(head)(ask_relay.start)
+    pl.when(z >= 2)(serve_prev)
 
     get_tap.wait()
     depth = kron.shape[1]
@@ -321,15 +338,21 @@
     pl.loop(1, rows // 2 - 1)(tap_rows)
     pl.when(relay)(send_lat)
 
+    @pl.when(second)
+    def _():
+        greet_prev()
+        serve_prev()
+
     @pl.when(relay)
     def _():
-        for k in (1, 0):
-            relayed[k].wait_recv()
-            heard(8 + k)
-            forward[k].start()
+        for copy in relayed:
+            copy.wait_recv()
+        heard(8)
+        forward.start()
 
     @pl.when(head)
     def _():
+        serve_next()
         heard(0, 4, 6)
         send(rims_prev)
 
@@ -429,10 +452,9 @@
 
     pl.when(head)(ask_relay.wait_send)
 
-    @pl.when(relay)
-    def _():
-        for copy in forward:
-            copy.wait_send()
+    pl.when(relay)(forward.wait_send)
+    pl.when(tail & odd)(give_pair.wait_send)
+    pl.when((z != WAVE - 1) | odd)(give_next.wait_send)
 
     @pl.when(z != 0)
     def _():
@@ -441,7 +463,6 @@
     ask_next.wait_send()
     for copy in rims:
         copy.wait_send()
-    give_next.wait_send()
     give_prev.wait_send()
 
 
@@ -474,13 +495,14 @@
             pltpu.SMEM((2, 2), jnp.int32),
             pltpu.SMEM((2, 2), jnp.int32),
             pltpu.SMEM((2, 2), jnp.int32),
+            pltpu.SMEM((2, 2), jnp.int32),
             pltpu.VMEM((channels * rows, columns), F32),
             pltpu.VMEM((rank, cells), BF16),
             pltpu.VMEM((rank, columns), BF16),
             pltpu.VMEM((6, rank, columns), BF16),
             pltpu.VMEM((rank, REACH * columns), BF16),
             pltpu.VMEM((rank, REACH * columns), BF16),
-            pltpu.VMEM((4, rank, width), BF16),
+            pltpu.VMEM((6, rank, width), BF16),
             pltpu.VMEM((4, rank, width), BF16),
             pltpu.VMEM((taps_rank * rank, depth), BF16),
             pltpu.VMEM((KS * rank, wide), BF16),
@@ -489,8 +511,8 @@
             pltpu.VMEM((rank, cells), F32),
             dma((12,)),
             dma((15,)),
-            dma((14,)),
-            pltpu.SemaphoreType.REGULAR((10,)),
+            dma((15,)),
+            pltpu.SemaphoreType.REGULAR((9,)),
         ],
         compiler_params=pltpu.CompilerParams(
             collective_id=0, has_side_effects=True, vmem_limit_bytes=56 * 1024 * 1024

time: 25.3 us -> 24.6 us (0.972)
  the two profiles are of different devices: /device:TPU:2 before, /device:TPU:1 now
where the time goes in v6:
time: 24.6 us; the launch traced here: 24.2 us
  Pallas kernels  23.5 us (96%)
  local copies, waits for them, and re-layouts  0.71 us (3%)
    pallas_call x1, Pallas kernels, on_device(): pl.pallas_call(functools.partial(kernel, n_lat, n_lon), out_shape=pltpu.V...  23.5 us
    unnamed x1, local copies, waits for them, and re-layouts  0.71 us

profile of v6, /device:TPU:1, one launch (start us, length us, event | category | flops | bytes accessed | tf_op | source)
XLA Modules:
  0.0 24.2 jit_solution(2841631231525816954)
XLA Ops:
  0.0 23.5 %layer.1 = bf16[64,16,128]{2,1,0:T(8,128)(2,1)S(1)} custom-call(bf16[64,16,128]{2,1,0:T(8,128)(2,1)} %feat_h.1, s32[16,128]{1,0:T(8,128)} %lab_h.1, s32[1,1,6]{2,1,0:T(1,128)} %tr_h.1, s32[5376]{0:T(1024)} %slot_h.1, bf16[112,32,512]{2,1,0:T(8,128)(2,1)} %bank_h.1, bf16[32,64]{1,0:T(8,128)(2,1)} %inf_h.1, bf16[16,25]{1,0:T(8,128)(2,1)} %tap_h.1, ...), custom_call_target="tpu_custom_call" | custom-call | tf_op jit(solution)/shard_map/layer/pallas_call | solution.py:480
  23.5 0.7 %copy.11 = bf16[64,16,128]{2,1,0:T(8,128)(2,1)} copy(bf16[64,16,128]{2,1,0:T(8,128)(2,1)S(1)} %layer.1) | data formatting | bytes 524288

commit v7 on v6

--- a/solution.py
+++ b/solution.py
@@ -27,7 +27,7 @@
     out_ref,
     feat_v, lab_v, tr_s, slot_s, bank_v, inf_v, tap_v, outf_v, bias_v,
     ask_s, asked_s, relay_s, relayed_s, spread, red, pack, packs, tops, bots, send_cores, cores,
-    kron, moved, rim_cells, tapped, held, local_sem, send_sem, recv_sem, hello,
+    kron, moved, rim_cells, tapped, held, blend, rim_window, local_sem, send_sem, recv_sem, hello,
 ):
     lat, lon = lax.axis_index("lat"), lax.axis_index("lon")
     up, down = lax.rem(lat + (n_lat - 1), n_lat), lax.rem(lat + 1, n_lat)
@@ -36,6 +36,14 @@
     rank = inf_v.shape[0]
     taps_rank = tap_v.shape[0]
     bank_rows = bank_v.shape[0]
+    def local(source, target, index):
+        copy = pltpu.make_async_copy(source, target, local_sem.at[index])
+        copy.start()
+        return copy
+
+    get_feat = local(feat_h, feat_v, 2)
+    get_inf = local(inf_h, inf_v, 3)
+
     z = lax.rem(lon, WAVE)
     head, tail, odd = z == 0, z == WAVE - 1, lax.rem(lat, 2) == 1
     even_lat = lax.rem(lat, 2) == 0
@@ -47,16 +55,6 @@
 
     second, middle = z == 1, (z >= 2) & (z <= WAVE - 2)
 
-    @pl.when((z >= 1) & (z < WAVE - 2))
-    def _():
-        for line in (lat, up, down):
-            signal(barrier, (line, nxt))
-
-    @pl.when(tail | second)
-    def _():
-        for line in (lat, up, down):
-            signal(barrier, (line, prev))
-
     round_trip = lambda steps: lax.rem(lon + steps + n_lon, n_lon)
     head_before, head_after = round_trip(-WAVE), round_trip(WAVE)
     my_tail, my_head = round_trip(WAVE - 1), round_trip(1 - WAVE)
@@ -73,11 +71,6 @@
         signal(barrier, (lat, my_tail))
         for line in (lat, up):
             signal(barrier, (line, head_after))
-
-    @pl.when(odd & (z != WAVE - 1))
-    def _():
-        for line in (up, down):
-            signal(barrier, (line, lon))
 
     @pl.when(tail)
     def _():
@@ -87,15 +80,23 @@
         signal(hello.at[6], (up, nxt))
         signal(hello.at[4], (down, nxt))
 
-    def local(source, target, index):
-        copy = pltpu.make_async_copy(source, target, local_sem.at[index])
-        copy.start()
-        return copy
+    @pl.when((z >= 1) & (z < WAVE - 2))
+    def _():
+        for line in (lat, up, down):
+            signal(barrier, (line, nxt))
+
+    @pl.when(tail | second)
+    def _():
+        for line in (lat, up, down):
+            signal(barrier, (line, prev))
+
+    @pl.when(odd & (z != WAVE - 1))
+    def _():
+        for line in (up, down):
+            signal(barrier, (line, lon))
 
     get_tr = local(tr_h, tr_s, 0)
     get_slot = local(slot_h, slot_s, 1)
-    get_feat = local(feat_h, feat_v, 2)
-    get_inf = local(inf_h, inf_v, 3)
     part = bank_rows // 4
     get_bank = [
         local(bank_h.at[pl.ds(i * part, part)], bank_v.at[pl.ds(i * part, part)], 8 + i) for i in range(4)
@@ -138,49 +139,6 @@
     def heard(*indices):
         for index in indices:
             pl.semaphore_wait(hello.at[index], 1)
-
-    get_tr.wait()
-    get_slot.wait()
-    slots = [slot_s[tr_s[0, 0, j]] for j in range(MAXR)]
-
-    def wanted(owner):
-        first = owner * bank_rows
-        row_a = row_b = at_a = at_b = count = jnp.int32(0)
-        for j in range(MAXR):
-            row = slots[j] - first
-            hit = (row >= 0) & (row < bank_rows)
-            is_a = hit & (count == 0)
-            is_b = hit & (count == 1)
-            row_a, at_a = jnp.where(is_a, row, row_a), jnp.where(is_a, j, at_a)
-            row_b, at_b = jnp.where(is_b, row, row_b), jnp.where(is_b, j, at_b)
-            count = count + hit.astype(jnp.int32)
-        return row_a, row_b, at_a, at_b
-
-    own_a, own_b, own_at, own_at_b = wanted(lon)
-    prev_a, prev_b, prev_at_a, prev_at_b = wanted(prev)
-    next_a, next_b, next_at_a, next_at_b = wanted(nxt)
-    ask_s[0, 0], ask_s[0, 1] = prev_a, prev_b
-    ask_s[1, 0], ask_s[1, 1] = next_a, next_b
-
-    ask_prev = remote(ask_s.at[0], asked_s.at[1], 0, (lat, prev))
-    ask_next = remote(ask_s.at[1], asked_s.at[0], 1, (lat, nxt))
-    ask_relay = remote(
-        ask_s.at[0], relay_s.at[lax.rem(lat, 2)], 12, (odd_lat, head_before), lands=12 + lax.rem(lat, 2)
-    )
-    relayed = [remote(ask_s.at[0], relay_s.at[k], 12, (odd_lat, head_before), lands=12 + k) for k in range(2)]
-    forward = remote(relay_s, relayed_s, 13, (lat, my_tail), lands=14)
-
-    pl.when(middle)(ask_prev.start)
-
-    @pl.when(head)
-    def _():
-        ask_relay.start()
-        ask_next.start()
-
-
-    @pl.when(tail)
-    def _():
-        ask_next.start()
 
     get_feat.wait()
     get_inf.wait()
@@ -219,6 +177,57 @@
     ]
     rims = rims_prev + rims_next + rims_lat
 
+    def send(copies):
+        for copy in copies:
+            copy.start()
+
+    @pl.when(head | tail)
+    def _():
+        send(rims_next)
+
+    get_tr.wait()
+    get_slot.wait()
+    slots = [slot_s[tr_s[0, 0, j]] for j in range(MAXR)]
+
+    def wanted(owner):
+        first = owner * bank_rows
+        row_a = row_b = at_a = at_b = count = jnp.int32(0)
+        for j in range(MAXR):
+            row = slots[j] - first
+            hit = (row >= 0) & (row < bank_rows)
+            is_a = hit & (count == 0)
+            is_b = hit & (count == 1)
+            row_a, at_a = jnp.where(is_a, row, row_a), jnp.where(is_a, j, at_a)
+            row_b, at_b = jnp.where(is_b, row, row_b), jnp.where(is_b, j, at_b)
+            count = count + hit.astype(jnp.int32)
+        return row_a, row_b, at_a, at_b
+
+    own_a, own_b, own_at, own_at_b = wanted(lon)
+    prev_a, prev_b, prev_at_a, prev_at_b = wanted(prev)
+    next_a, next_b, next_at_a, next_at_b = wanted(nxt)
+    ask_s[0, 0], ask_s[0, 1] = prev_a, prev_b
+    ask_s[1, 0], ask_s[1, 1] = next_a, next_b
+
+    ask_prev = remote(ask_s.at[0], asked_s.at[1], 0, (lat, prev))
+    ask_next = remote(ask_s.at[1], asked_s.at[0], 1, (lat, nxt))
+    ask_relay = remote(
+        ask_s.at[0], relay_s.at[lax.rem(lat, 2)], 12, (odd_lat, head_before), lands=12 + lax.rem(lat, 2)
+    )
+    relayed = [remote(ask_s.at[0], relay_s.at[k], 12, (odd_lat, head_before), lands=12 + k) for k in range(2)]
+    forward = remote(relay_s, relayed_s, 13, (lat, my_tail), lands=14)
+
+    pl.when(middle)(ask_prev.start)
+
+    @pl.when(head)
+    def _():
+        ask_relay.start()
+        ask_next.start()
+
+
+    @pl.when(tail)
+    def _():
+        ask_next.start()
+
     give_next = remote(send_cores.at[pl.ds(0, 2)], cores.at[pl.ds(0, 2)], 10, (lat, nxt))
     give_prev = remote(send_cores.at[pl.ds(2, 2)], cores.at[pl.ds(2, 2)], 11, (lat, prev))
 
@@ -244,14 +253,6 @@
         send_cores[2] = bank_v[asked_s[0, 0]]
         send_cores[3] = bank_v[asked_s[0, 1]]
         give_prev.start()
-
-    def send(copies):
-        for copy in copies:
-            copy.start()
-
-    @pl.when(head | tail)
-    def _():
-        send(rims_next)
 
     @pl.when(middle)
     def _():
@@ -353,8 +354,6 @@
     @pl.when(head)
     def _():
         serve_next()
-        heard(0, 4, 6)
-        send(rims_prev)
 
     for copy in rims_lat:
         copy.wait_recv()
@@ -376,6 +375,7 @@
         hidden = jnp.where(label == next_at_a, theirs[:rank], hidden)
         held[:, pl.ds(start, 2 * span)] = jnp.where(label == next_at_b, theirs[rank:], hidden)
 
+    blend[...] = dot(jnp.concatenate([own_cores, next_cores], axis=0), kron[...]).astype(BF16)
     get_outf.wait()
     get_bias.wait()
     square = (channels, channels)
@@ -389,17 +389,21 @@
     )
     rim_label = jnp.broadcast_to(rim_label, (rank, LANES))
 
-    pl.when(head)(serve_prev)
+    @pl.when(head)
+    def _():
+        heard(0, 4, 6)
+        send(rims_prev)
+        serve_prev()
 
     for copy in rims_prev + rims_next:
         copy.wait_recv()
     even = lane % 4 < 2
-    middle, above, below = (
+    beside, above, below = (
         jnp.where(even, packs[2 * k].astype(F32), packs[2 * k + 1].astype(F32)) for k in range(3)
     )
     above = pltpu.roll(above, LANES // 2, 1) * not_first
     below = pltpu.roll(below, LANES // 2, 1) * not_last
-    sides = jnp.where(lane < 4 * REACH, above, jnp.where(lane < 4 * (rows + REACH), middle, below))
+    sides = jnp.where(lane < 4 * REACH, above, jnp.where(lane < 4 * (rows + REACH), beside, below))
     spot = lane % 4
     fixed = (
         jnp.where(spot >= 2, pltpu.roll(sides, 2, 1), rim_cells[0]),
@@ -413,34 +417,31 @@
         for dy in range(KS)
         for dx in range(KS)
     ]
-    rim_tapped = dot(kron[...], jnp.concatenate(pieces + [blank[:, :LANES]], axis=0)).astype(BF16)
-    ready = jnp.concatenate([own_cores, next_cores], axis=0)
-    theirs = dot(ready, rim_tapped)
+    rim_window[...] = jnp.concatenate(pieces + [blank[:, :LANES]], axis=0)
+    theirs = dot(blend[...], rim_window[...])
     rim_hidden = theirs[:rank]
     for k, at in enumerate((own_at_b, next_at_a, next_at_b)):
         rim_hidden = jnp.where(rim_label == at, theirs[(k + 1) * rank : (k + 2) * rank], rim_hidden)
 
     give_next.wait_recv()
     prev_cores = cores[pl.ds(0, 2)].reshape(2 * rank, cores.shape[2])
-    last = outf_v[...]
-    theirs = dot(prev_cores, rim_tapped)
+    theirs = dot(dot(prev_cores, kron[...]).astype(BF16), rim_window[...])
     rim_hidden = jnp.where(rim_label == prev_at_a, theirs[:rank], rim_hidden)
     rim_hidden = jnp.where(rim_label == prev_at_b, theirs[rank:], rim_hidden)
+    last = outf_v[...]
     at_rim = (lane < REACH) | (lane >= LANES - REACH)
     group = 4
     for first in range(0, rows, group):
-        width = group * LANES
-        theirs = dot(prev_cores, tapped[:, first * LANES : first * LANES + width])
+        theirs = dot(prev_cores, tapped[:, first * LANES : (first + group) * LANES])
         parts = []
         for k in range(group):
             r = first + k
             label = label_row(r)
             mine = slice(k * LANES, (k + 1) * LANES)
-            hidden = held[:, r * LANES : (r + 1) * LANES]
-            hidden = jnp.where(label == prev_at_a, theirs[:rank, mine], hidden)
+            hidden = jnp.where(label == prev_at_a, theirs[:rank, mine], held[:, r * LANES : (r + 1) * LANES])
             hidden = jnp.where(label == prev_at_b, theirs[rank:, mine], hidden)
-            beside = pltpu.roll(rim_hidden, (LANES - 2 - 4 * r) % LANES, 1)
-            parts.append(jnp.where(at_rim, beside, hidden).astype(BF16))
+            here = pltpu.roll(rim_hidden, (LANES - 2 - 4 * r) % LANES, 1)
+            parts.append(jnp.where(at_rim, here, hidden).astype(BF16))
         value = lax.dot_general(
             last, jnp.concatenate(parts, axis=1), (((0,), (0,)), ((), ())), preferred_element_type=F32
         ) + bias
@@ -509,6 +510,8 @@
             pltpu.VMEM((KS, rank, columns), F32),
             pltpu.VMEM((taps_rank * rank, cells), BF16),
             pltpu.VMEM((rank, cells), F32),
+            pltpu.VMEM((4 * rank, depth), BF16),
+            pltpu.VMEM((depth, columns), BF16),
             dma((12,)),
             dma((15,)),
             dma((15,)),

time: 24.6 us -> 24.1 us (0.980); the launches traced: 24.2 us -> 24 us
  no operation moved by 1% of the time
where the time goes in v7:
time: 24.1 us; the launch traced here: 24 us
  Pallas kernels  23.3 us (97%)
  local copies, waits for them, and re-layouts  0.71 us (3%)
    pallas_call x1, Pallas kernels, on_device(): pl.pallas_call(functools.partial(kernel, n_lat, n_lon), out_shape=pltpu.V...  23.3 us
    unnamed x1, local copies, waits for them, and re-layouts  0.71 us

profile of v7, /device:TPU:1, one launch (start us, length us, event | category | flops | bytes accessed | tf_op | source)
XLA Modules:
  0.0 24.0 jit_solution(8047484227235786057)
XLA Ops:
  0.0 23.3 %layer.1 = bf16[64,16,128]{2,1,0:T(8,128)(2,1)S(1)} custom-call(bf16[64,16,128]{2,1,0:T(8,128)(2,1)} %feat_h.1, s32[16,128]{1,0:T(8,128)} %lab_h.1, s32[1,1,6]{2,1,0:T(1,128)} %tr_h.1, s32[5376]{0:T(1024)} %slot_h.1, bf16[112,32,512]{2,1,0:T(8,128)(2,1)} %bank_h.1, bf16[32,64]{1,0:T(8,128)(2,1)} %inf_h.1, bf16[16,25]{1,0:T(8,128)(2,1)} %tap_h.1, ...), custom_call_target="tpu_custom_call" | custom-call | tf_op jit(solution)/shard_map/layer/pallas_call | solution.py:481
  23.3 0.7 %copy.11 = bf16[64,16,128]{2,1,0:T(8,128)(2,1)} copy(bf16[64,16,128]{2,1,0:T(8,128)(2,1)S(1)} %layer.1) | data formatting | bytes 524288

commit v8 on v7

--- a/solution.py
+++ b/solution.py
@@ -430,7 +430,7 @@
     rim_hidden = jnp.where(rim_label == prev_at_b, theirs[rank:], rim_hidden)
     last = outf_v[...]
     at_rim = (lane < REACH) | (lane >= LANES - REACH)
-    group = 4
+    group = 16
     for first in range(0, rows, group):
         theirs = dot(prev_cores, tapped[:, first * LANES : (first + group) * LANES])
         parts = []

time: 24.1 us -> 23.7 us (0.983)
  Pallas kernels: 23.3 us -> 22.9 us
    pallas_call x1, Pallas kernels: 23.3 us -> 22.9 us  [on_device(): pl.pallas_call(functools.partial(kernel, n_lat, n_lon), out_shape=pltpu.V...]
where the time goes in v8:
time: 23.7 us; the launch traced here: 23.6 us
  Pallas kernels  22.9 us (97%)
  local copies, waits for them, and re-layouts  0.71 us (3%)
    pallas_call x1, Pallas kernels, on_device(): pl.pallas_call(functools.partial(kernel, n_lat, n_lon), out_shape=pltpu.V...  22.9 us
    unnamed x1, local copies, waits for them, and re-layouts  0.71 us

profile of v8, /device:TPU:1, one launch (start us, length us, event | category | flops | bytes accessed | tf_op | source)
XLA Modules:
  0.0 23.6 jit_solution(503767418512135589)
XLA Ops:
  0.0 22.9 %layer.1 = bf16[64,16,128]{2,1,0:T(8,128)(2,1)S(1)} custom-call(bf16[64,16,128]{2,1,0:T(8,128)(2,1)} %feat_h.1, s32[16,128]{1,0:T(8,128)} %lab_h.1, s32[1,1,6]{2,1,0:T(1,128)} %tr_h.1, s32[5376]{0:T(1024)} %slot_h.1, bf16[112,32,512]{2,1,0:T(8,128)(2,1)} %bank_h.1, bf16[32,64]{1,0:T(8,128)(2,1)} %inf_h.1, bf16[16,25]{1,0:T(8,128)(2,1)} %tap_h.1, ...), custom_call_target="tpu_custom_call" | custom-call | tf_op jit(solution)/shard_map/layer/pallas_call | solution.py:481
  22.9 0.7 %copy.11 = bf16[64,16,128]{2,1,0:T(8,128)(2,1)} copy(bf16[64,16,128]{2,1,0:T(8,128)(2,1)S(1)} %layer.1) | data formatting | bytes 524288
